TPU v7x, 32 devices: a whole 2x2x4 slice. The times are simulated.
32 devices in a mesh: row: 16 (over z, x, core), col: 2 (over y).
Axes of the slice: x: 2, y: 2, z: 4, core: 2. Of those that a mesh axis runs over, the one named last changes fastest.
Arguments:
- polar_rays: bfloat16 [32, 360, 256], P(('row', 'col')), may hold values from -6 to 6
- first_line: int32 [32, 16, 2], P('row', None, 'col'), may hold values from 0 to 359
- second_line: int32 [32, 16, 2], P('row', None, 'col'), may hold values from 0 to 179
- start_frame: float32 [3, 3, 32], P(None, None, ('row', 'col')), may hold values from -6 to 6
Outputs:
- line_scores: float32 [32, 16, 2], P('row', None, 'col')
- estimates: float32 [3, 3, 32], P(None, None, ('row', 'col'))
All inputs are finite; a program needn't handle non-finite values. Where the computation divides by a largest or mean magnitude, that divisor is 1e-20 or more.
Results may differ from a plain program's by a relative error of at most 0.0003.
Values may be sent and summed in bfloat16 or wider, within the bound.
No kernel may reach another device: no remote copies, remote signals or barrier semaphores. Data moves between devices by JAX's collectives and lax.ppermute only.
A program may use at most 64 MiB of HBM per device.

v0:
```python
import functools
import math

import jax
import jax.numpy as jnp
from jax import lax
from jax.experimental import pallas as pl
from jax.experimental.pallas import tpu as pltpu
from jax.sharding import PartitionSpec as P

ITERS = 3
LANES = 128
SCORE_VMEM = 24 << 20
POWER_VMEM = 16 << 20
PAIR = 2


class Plan:
    def __init__(self, rows, cols):
        self.rows, self.cols = rows, cols
        self.depth = rows // (PAIR * PAIR)
        self.count = rows * cols
        self.firsts = PAIR * cols
        self.seconds = PAIR * self.depth
        self.pairs = self.firsts * self.seconds
        self.width = -(-(3 * self.pairs + 9) // LANES) * LANES
        self.table = -(-2 * self.rows * self.cols // LANES) * LANES

    def flat(self, z, x, core, c):
        return ((z * PAIR + x) * PAIR + core) * self.cols + c


def position():
    row, c = lax.axis_index("row"), lax.axis_index("col")
    return row // (PAIR * PAIR), (row // PAIR) % PAIR, row % PAIR, c


def prepare_kernel(plan, half, rays_ref, first_ref, second_ref, half_ref, table_ref, sem):
    copy = pltpu.make_async_copy(rays_ref.at[:, pl.ds(0, half)], half_ref, sem)
    copy.start()
    parts = [first_ref[c] for c in range(plan.cols)] + [second_ref[c] for c in range(plan.cols)]
    spare = plan.table - 2 * plan.rows * plan.cols
    if spare:
        parts.append(jnp.zeros((1, spare), jnp.int32))
    table_ref[...] = jnp.concatenate(parts, axis=1)
    copy.wait()


def score_kernel(plan, rays, half, *refs):
    fulls = refs[: plan.firsts]
    halves = refs[plan.firsts : plan.firsts + plan.seconds]
    own_table, next_table, start_ref, message_ref = refs[plan.firsts + plan.seconds : -6]
    full_rows, half_rows, first_rows, second_rows, parts, means = refs[-6:]
    z, x, core, c = position()
    scale = 1.0 / (rays * half)

    full_sums, half_sums = [], []
    for n, ref in enumerate(fulls):
        values = ref[0].astype(jnp.float32)
        full_rows[n] = values
        full_sums.append(jnp.sum(values, axis=0, keepdims=True))
    for n, ref in enumerate(halves):
        values = ref[0, :half].astype(jnp.float32)
        half_rows[n] = values
        half_sums.append(jnp.sum(values, axis=0, keepdims=True))
    half_sum = jnp.concatenate(half_sums, axis=0)
    for n in range(plan.firsts):
        means[pl.ds(n * plan.seconds, plan.seconds), :] = jnp.broadcast_to(
            jnp.sum(half_sum * full_sums[n], axis=1, keepdims=True) * scale, (plan.seconds, LANES)
        )

    lane = lax.broadcasted_iota(jnp.int32, (1, plan.width), 1)
    lines = jnp.zeros((1, plan.width), jnp.int32)
    own_slot = (((x * plan.cols + c) * plan.depth) + z) * PAIR + core
    for n in range(plan.firsts):
        dx, dc = n // plan.cols, n % plan.cols
        table = next_table if dx else own_table
        for m in range(plan.seconds):
            dz, dk = m // PAIR, m % PAIR
            pair = n * plan.seconds + m
            at = (c ^ dc) * plan.rows + ((z ^ dz) * PAIR + x) * PAIR + (core ^ dk)
            a = table[0, at]
            b = table[0, plan.rows * plan.cols + at]
            first_rows[pl.ds(pair, 1), :] = full_rows[n, pl.ds(a, 1), :]
            second_rows[pl.ds(pair, 1), :] = half_rows[m, pl.ds(b, 1), :]
            slot = own_slot ^ pair
            lines = jnp.where(lane == plan.pairs + slot, a, lines)
            lines = jnp.where(lane == 2 * plan.pairs + slot, b, lines)
            corr = lax.dot_general(
                halves[m][0, :half], fulls[n][0], (((1,), (1,)), ((), ())), preferred_element_type=jnp.float32
            )
            center = means[pl.ds(pair, 1), 0:1]
            parts[pl.ds(pair, 1), :] = jnp.sum(jnp.abs(corr - center), axis=0, keepdims=True)

    center = means[:, 0:1]
    spread = jnp.sum(parts[...], axis=1, keepdims=True) * scale
    picked = jnp.sum(first_rows[...] * second_rows[...], axis=1, keepdims=True)
    score = (picked - center) / (spread + 1e-05)
    wide = (plan.pairs, plan.width)
    to = own_slot ^ lax.broadcasted_iota(jnp.int32, wide, 0)
    here = lax.broadcasted_iota(jnp.int32, wide, 1) == to
    message = jnp.sum(jnp.where(here, score, 0.0), axis=0, keepdims=True) + lines.astype(jnp.float32)
    for k in range(3):
        for q in range(3):
            message = jnp.where(lane == 3 * plan.pairs + 3 * k + q, start_ref[k, 0, q], message)
    message_ref[...] = jnp.broadcast_to(message[None], message_ref.shape)


def power_kernel(plan, rays, gathered_ref, scores_ref, frames_ref, rows_ref, sorted_ref, matrix_ref):
    z, x, core, c = position()
    count, seconds = plan.count, plan.seconds
    for device in range(count):
        dz, rest = divmod(device, PAIR * PAIR * plan.cols)
        dx, rest = divmod(rest, PAIR * plan.cols)
        dk, dc = divmod(rest, plan.cols)
        rows_ref[pl.ds((dx * plan.cols + dc) * seconds + dz * PAIR + dk, 1), :] = gathered_ref[device]

    lane = lax.broadcasted_iota(jnp.int32, (seconds, plan.width), 1)
    block = (lane // seconds) % plan.firsts
    for to in range(plan.firsts):
        mixed = jnp.zeros((seconds, plan.width), jnp.float32)
        for b in range(plan.firsts):
            moved = rows_ref[b * seconds : (b + 1) * seconds, :]
            if b != to:
                moved = jnp.roll(moved, (b - to) * seconds, axis=1)
            mixed = jnp.where(block == b, moved, mixed)
        sorted_ref[to * seconds : (to + 1) * seconds, :] = mixed

    score = sorted_ref[:, :count]
    turn = 2.0 * math.pi / rays
    first = sorted_ref[:, count : 2 * count] * turn
    second = sorted_ref[:, 2 * count : 3 * count] * turn
    weighted = jnp.concatenate([score * jnp.cos(second), score * jnp.sin(second), score], axis=1)
    for p, unit in enumerate((jnp.cos(first), jnp.sin(first))):
        matrix_ref[p * count : (p + 1) * count, :] = weighted * jnp.concatenate([unit] * 3, axis=1)
    matrix_ref[2 * count :, :] = weighted

    begin = 3 * plan.pairs
    tile = begin // LANES * LANES
    turned = jnp.transpose(rows_ref[:, tile : tile + LANES])
    at = begin - tile
    frames = [
        jnp.concatenate([turned[at + 3 * k + q : at + 3 * k + q + 1] for q in range(3)], axis=1) for k in range(3)
    ]
    pad = jnp.zeros((5, 3 * count), jnp.float32)
    for _ in range(ITERS):
        stacked = jnp.concatenate(frames + [pad], axis=0)
        mixed = lax.dot_general(
            stacked,
            matrix_ref[...],
            (((1,), (1,)), ((), ())),
            precision=lax.Precision.HIGHEST,
            preferred_element_type=jnp.float32,
        )
        y = [mixed[k : k + 1] for k in range(3)]

        def gram(k, l):
            return jnp.sum(y[k] * y[l], axis=1, keepdims=True)

        f00 = jnp.sqrt(gram(0, 0))
        f10 = gram(1, 0) / f00
        f20 = gram(2, 0) / f00
        f11 = jnp.sqrt(gram(1, 1) - f10 * f10)
        f21 = (gram(2, 1) - f20 * f10) / f11
        f22 = jnp.sqrt(gram(2, 2) - f20 * f20 - f21 * f21)
        v0 = y[0] / f00
        v1 = (y[1] - f10 * v0) / f11
        v2 = (y[2] - f20 * v0 - f21 * v1) / f22
        frames = [v0, v1, v2]

    own = (x * plan.cols + c) * seconds + z * PAIR + core
    wide = lax.broadcasted_iota(jnp.int32, (1, 3 * count), 1)
    three = lax.broadcasted_iota(jnp.int32, (1, 3), 1)
    for k in range(3):
        out = jnp.zeros((1, 3), jnp.float32)
        for q in range(3):
            value = jnp.sum(jnp.where(wide == q * count + own, frames[k], 0.0), axis=1, keepdims=True)
            out = jnp.where(three == q, value, out)
        frames_ref[k] = math.sqrt(count) * out

    source = lax.broadcasted_iota(jnp.int32, (seconds, plan.rows), 0)
    target = lax.broadcasted_iota(jnp.int32, (seconds, plan.rows), 1)
    lines = [jnp.zeros((1, plan.rows), jnp.float32) for _ in range(plan.cols)]
    for dx in range(PAIR):
        row = rows_ref[pl.ds((dx * plan.cols + c) * seconds + z * PAIR + core, 1), :]
        spread = (target == (source // PAIR) * (PAIR * PAIR) + dx * PAIR + source % PAIR).astype(jnp.float32)
        for dc in range(plan.cols):
            low = row[:, dc * seconds : (dc + 1) * seconds]
            high = row[:, (plan.cols + dc) * seconds : (plan.cols + dc + 1) * seconds]
            part = jnp.broadcast_to(jnp.where(x == 1, high, low), (8, seconds))
            moved = lax.dot_general(
                part,
                spread,
                (((1,), (0,)), ((), ())),
                precision=lax.Precision.HIGHEST,
                preferred_element_type=jnp.float32,
            )
            lines[dc] = lines[dc] + moved[0:1]
    for dc in range(plan.cols):
        scores_ref[dc] = lines[dc]


def scored(plan, polar_rays, first_line, second_line, start_frame):
    _, rays, depth = polar_rays.shape
    half = rays // 2
    half_tiled = -(-half // 8) * 8
    axes = ("row", "col")
    vmem = pl.BlockSpec(memory_space=pltpu.VMEM)
    smem = pl.BlockSpec(memory_space=pltpu.SMEM)
    anywhere = pl.BlockSpec(memory_space=pl.ANY)

    def swap(value, distance):
        return lax.ppermute(value, axes, [(n, n ^ distance) for n in range(plan.count)])

    first = jnp.transpose(first_line, (0, 2, 1))
    second = jnp.transpose(second_line, (0, 2, 1))
    half_rays, own_table = pl.pallas_call(
        functools.partial(prepare_kernel, plan, half_tiled),
        out_shape=(
            jax.ShapeDtypeStruct((1, half_tiled, depth), polar_rays.dtype),
            jax.ShapeDtypeStruct((1, plan.table), jnp.int32),
        ),
        in_specs=[anywhere, vmem, vmem],
        out_specs=(vmem, vmem),
        scratch_shapes=[pltpu.SemaphoreType.DMA],
        compiler_params=pltpu.CompilerParams(vmem_limit_bytes=1 << 20),
        name="prepare",
    )(polar_rays, first, second)

    next_table = swap(own_table, plan.flat(0, 1, 0, 0))
    fulls = [polar_rays] + [
        swap(polar_rays, plan.flat(0, n // plan.cols, 0, n % plan.cols)) for n in range(1, plan.firsts)
    ]
    deep = [half_rays] + [swap(half_rays, plan.flat(dz, 0, 0, 0)) for dz in range(1, plan.depth)]
    halves = []
    for piece in deep:
        halves += [piece, swap(piece, plan.flat(0, 0, 1, 0))]

    message = pl.pallas_call(
        functools.partial(score_kernel, plan, rays, half),
        out_shape=jax.ShapeDtypeStruct((plan.count, 1, plan.width), jnp.float32),
        in_specs=[vmem] * (plan.firsts + plan.seconds) + [smem, smem, smem],
        out_specs=vmem,
        compiler_params=pltpu.CompilerParams(vmem_limit_bytes=SCORE_VMEM),
        scratch_shapes=[
            pltpu.VMEM((plan.firsts, rays, depth), jnp.float32),
            pltpu.VMEM((plan.seconds, half, depth), jnp.float32),
            pltpu.VMEM((plan.pairs, depth), jnp.float32),
            pltpu.VMEM((plan.pairs, depth), jnp.float32),
            pltpu.VMEM((plan.pairs, rays), jnp.float32),
            pltpu.VMEM((plan.pairs, LANES), jnp.float32),
        ],
        name="score",
    )(*fulls, *halves, own_table, next_table, jnp.transpose(start_frame, (0, 2, 1)))

    gathered = lax.all_to_all(message, axes, 0, 0, tiled=True)

    scores, frames = pl.pallas_call(
        functools.partial(power_kernel, plan, rays),
        out_shape=(
            jax.ShapeDtypeStruct((plan.cols, 1, plan.rows), jnp.float32),
            jax.ShapeDtypeStruct((3, 1, 3), jnp.float32),
        ),
        in_specs=[vmem],
        out_specs=(vmem, vmem),
        compiler_params=pltpu.CompilerParams(vmem_limit_bytes=POWER_VMEM),
        scratch_shapes=[
            pltpu.VMEM((plan.count, plan.width), jnp.float32),
            pltpu.VMEM((plan.count, plan.width), jnp.float32),
            pltpu.VMEM((3 * plan.count, 3 * plan.count), jnp.float32),
        ],
        name="power",
    )(gathered)
    return jnp.transpose(scores, (0, 2, 1)), jnp.transpose(frames, (0, 2, 1))


def per_device(plan, *arrays):
    return scored(plan, *arrays)


def solution(mesh):
    plan = Plan(mesh.shape["row"], mesh.shape["col"])
    placed = (
        P(("row", "col"), None, None),
        P("row", None, "col"),
        P("row", None, "col"),
        P(None, None, ("row", "col")),
    )
    return jax.shard_map(
        functools.partial(per_device, plan),
        mesh=mesh,
        in_specs=placed,
        out_specs=(P("row", None, "col"), P(None, None, ("row", "col"))),
        check_vma=False,
    )
```

profile of v0, /device:TPU:0, one launch (start us, length us, event | category | flops | bytes accessed | tf_op | source)
XLA Modules:
  0.0 38.6 jit_solution(6195331626419775779)
XLA Ops:
  0.6 0.7 %copy-done.4 = s32[2,16,1]{1,2,0:T(1,128)S(1)} copy-done((s32[2,16,1]{1,2,0:T(1,128)S(1)}, s32[2,16,1]{1,2,0:T(1,128)}, u32[]{:S(2)}) %copy-start.4) | copy-done | bytes 152
  1.3 0.0 copy-done.3
  1.3 0.9 %copy-done = bf16[1,360,256]{2,1,0:T(8,128)(2,1)S(1)} copy-done((bf16[1,360,256]{2,1,0:T(8,128)(2,1)S(1)}, bf16[1,360,256]{2,1,0:T(8,128)(2,1)}, u32[]{:S(2)}) %copy-start) | copy-done | bytes 184344
  2.3 0.2 prepare.1
  2.4 0.0 copy-start.2
  2.5 5.1 %collective-permute-start.8 = (bf16[1,184,256]{2,1,0:T(8,128)(2,1)S(1)}, bf16[1,184,256]{2,1,0:T(8,128)(2,1)S(1)}, u32[]{:S(2)}, u32[]{:S(2)}) collective-permute-start(bf16[1,184,256]{2,1,0:T(8,128)(2,1)S(1)} %get-tuple-element.6.refs_4_), channel_id=1, source_target_pairs={{0,24},{1,25},{2,26},{3,27},{4,28},{5,29},{6,30},{7,31},{8,16},{9,... | collective-permute-start | bytes 282632 | tf_op jit(solution)/shard_map/ppermute | solution.py:213
  7.6 0.0 collective-permute-start.6
  7.6 2.4 %collective-permute-start.2 = (bf16[1,360,256]{2,1,0:T(8,128)(2,1)S(1)}, bf16[1,360,256]{2,1,0:T(8,128)(2,1)S(1)}, u32[]{:S(2)}, u32[]{:S(2)}) collective-permute-start(bf16[1,360,256]{2,1,0:T(8,128)(2,1)S(1)} %copy-done.1), channel_id=1, source_target_pairs={{0,5},{1,4},{2,7},{3,6},{4,1},{5,0},{6,3},{7,2},{8,13},{9,12},{10,... | collective-permute-start | bytes 552968 | tf_op jit(solution)/shard_map/ppermute | solution.py:213
  10.1 0.5 %collective-permute-start.10 = (s32[1,128]{1,0:T(1,128)S(1)}, s32[1,128]{1,0:T(1,128)S(1)}, u32[]{:S(2)}, u32[]{:S(2)}) collective-permute-start(s32[1,128]{1,0:T(1,128)S(1)} %get-tuple-element.7.refs_12_), channel_id=1, source_target_pairs={{0,4},{1,5},{2,6},{3,7},{4,0},{5,1},{6,2},{7,3},{8,12},{9,13},{10,... | collective-permute-start | bytes 1544 | tf_op jit(solution)/shard_map/ppermute | solution.py:213
  10.6 0.8 %collective-permute-start.4 = (bf16[1,184,256]{2,1,0:T(8,128)(2,1)S(1)}, bf16[1,184,256]{2,1,0:T(8,128)(2,1)S(1)}, u32[]{:S(2)}, u32[]{:S(2)}) collective-permute-start(bf16[1,184,256]{2,1,0:T(8,128)(2,1)S(1)} %get-tuple-element.6.refs_4_), channel_id=1, source_target_pairs={{0,8},{1,9},{2,10},{3,11},{4,12},{5,13},{6,14},{7,15},{8,0},{9,1},... | collective-permute-start | bytes 282632 | tf_op jit(solution)/shard_map/ppermute | solution.py:213
  11.4 3.3 %collective-permute-done.10.refs_13_ = s32[1,128]{1,0:T(1,128)S(1)} collective-permute-done((s32[1,128]{1,0:T(1,128)S(1)}, s32[1,128]{1,0:T(1,128)S(1)}, u32[]{:S(2)}, u32[]{:S(2)}) %collective-permute-start.10) | collective-permute-done | bytes 544 | tf_op jit(solution)/shard_map/ppermute | solution.py:213
  14.7 0.0 collective-permute-start.3
  14.7 0.0 collective-permute-done.8.refs_10_
  14.7 1.5 %collective-permute-start.1 = (bf16[1,360,256]{2,1,0:T(8,128)(2,1)S(1)}, bf16[1,360,256]{2,1,0:T(8,128)(2,1)S(1)}, u32[]{:S(2)}, u32[]{:S(2)}) collective-permute-start(bf16[1,360,256]{2,1,0:T(8,128)(2,1)S(1)} %copy-done.1), channel_id=1, source_target_pairs={{0,4},{1,5},{2,6},{3,7},{4,0},{5,1},{6,2},{7,3},{8,12},{9,13},{10,... | collective-permute-start | bytes 552968 | tf_op jit(solution)/shard_map/ppermute | solution.py:213
  16.2 1.0 %collective-permute-start = (bf16[1,360,256]{2,1,0:T(8,128)(2,1)S(1)}, bf16[1,360,256]{2,1,0:T(8,128)(2,1)S(1)}, u32[]{:S(2)}, u32[]{:S(2)}) collective-permute-start(bf16[1,360,256]{2,1,0:T(8,128)(2,1)S(1)} %copy-done.1), channel_id=1, source_target_pairs={{0,1},{1,0},{2,3},{3,2},{4,5},{5,4},{6,7},{7,6},{8,9},{9,8},{10,11... | collective-permute-start | bytes 552968 | tf_op jit(solution)/shard_map/ppermute | solution.py:213
  17.1 0.5 %collective-permute-start.7 = (bf16[1,184,256]{2,1,0:T(8,128)(2,1)S(1)}, bf16[1,184,256]{2,1,0:T(8,128)(2,1)S(1)}, u32[]{:S(2)}, u32[]{:S(2)}) collective-permute-start(bf16[1,184,256]{2,1,0:T(8,128)(2,1)S(1)} %collective-permute-done.6.refs_8_), channel_id=1, source_target_pairs={{0,2},{1,3},{2,0},{3,1},{4,6},{5,7},{6,4},{7,5},{8,10},{9,11},{10,... | collective-permute-start | bytes 282632 | tf_op jit(solution)/shard_map/ppermute | solution.py:213
  17.7 0.1 collective-permute-start.5
  17.7 4.0 %collective-permute-done.1.refs_2_ = bf16[1,360,256]{2,1,0:T(8,128)(2,1)S(1)} collective-permute-done((bf16[1,360,256]{2,1,0:T(8,128)(2,1)S(1)}, bf16[1,360,256]{2,1,0:T(8,128)(2,1)S(1)}, u32[]{:S(2)}, u32[]{:S(2)}) %collective-permute-start.1) | collective-permute-done | bytes 184352 | tf_op jit(solution)/shard_map/ppermute | solution.py:213
  21.7 1.2 %collective-permute-done.refs_1_ = bf16[1,360,256]{2,1,0:T(8,128)(2,1)S(1)} collective-permute-done((bf16[1,360,256]{2,1,0:T(8,128)(2,1)S(1)}, bf16[1,360,256]{2,1,0:T(8,128)(2,1)S(1)}, u32[]{:S(2)}, u32[]{:S(2)}) %collective-permute-start) | collective-permute-done | bytes 184352 | tf_op jit(solution)/shard_map/ppermute | solution.py:213
  22.9 0.0 collective-permute-done.9.refs_11_
  22.9 0.0 collective-permute-done.7.refs_9_
  23.0 3.4 %score.1 = f32[32,1,128]{2,1,0:T(1,128)S(1)} custom-call(bf16[1,360,256]{2,1,0:T(8,128)(2,1)S(1)} %copy-done.1, bf16[1,360,256]{2,1,0:T(8,128)(2,1)S(1)} %collective-permute-done.refs_1_, bf16[1,360,256]{2,1,0:T(8,128)(2,1)S(1)} %collective-permute-done.1.refs_2_, bf16[1,360,256]{2,1,0:T(8,128)(2,1)S(1)} %collective-permute-done.2.refs_3_, ...), custom_call_target="tpu_custom_call" | custom-call | tf_op jit(solution)/shard_map/score/pallas_call | solution.py:239
  26.3 10.0 %all_to_all.5.gathered_ref = f32[32,1,128]{2,1,0:T(1,128)S(1)} all-to-all(f32[32,1,128]{2,1,0:T(1,128)S(1)} %score.1), channel_id=1, replica_groups=mesh['row'=16,'col'=2] {'row','col'}, dimensions={0} | all-to-all | bytes 32768 | tf_op jit(solution)/shard_map/all_to_all | solution.py:256
  36.4 2.2 %power.1 = (f32[2,1,16]{2,1,0:T(1,128)}, f32[3,1,3]{2,1,0:T(1,128)}) custom-call(f32[32,1,128]{2,1,0:T(1,128)S(1)} %all_to_all.5.gathered_ref), custom_call_target="tpu_custom_call" | custom-call | tf_op jit(solution)/shard_map/power/pallas_call | solution.py:258
  (12 shorter events, 0.0 us)
Async XLA Ops:
  0.6 0.7 %copy-start.4 = (s32[2,16,1]{1,2,0:T(1,128)S(1)}, s32[2,16,1]{1,2,0:T(1,128)}, u32[]{:S(2)}) copy-start(s32[2,16,1]{1,2,0:T(1,128)} %param.6) | copy-start | bytes 388
  0.6 0.7 %copy-start.3 = (s32[2,16,1]{1,2,0:T(1,128)S(1)}, s32[2,16,1]{1,2,0:T(1,128)}, u32[]{:S(2)}) copy-start(s32[2,16,1]{1,2,0:T(1,128)} %param.5) | copy-start | bytes 388
  1.3 0.9 %copy-start = (bf16[1,360,256]{2,1,0:T(8,128)(2,1)S(1)}, bf16[1,360,256]{2,1,0:T(8,128)(2,1)}, u32[]{:S(2)}) copy-start(bf16[1,360,256]{2,1,0:T(8,128)(2,1)} %refs_0_.1) | copy-start | bytes 552964
  2.2 5.4 %copy-start.1 = (bf16[1,360,256]{2,1,0:T(8,128)(2,1)S(1)}, bf16[1,360,256]{2,1,0:T(8,128)(2,1)}, u32[]{:S(2)}) copy-start(bf16[1,360,256]{2,1,0:T(8,128)(2,1)} %refs_0_.1) | copy-start | bytes 552964
  2.4 20.5 %copy-start.2 = (f32[3,3,1]{1,2,0:T(1,128)S(1)}, f32[3,3,1]{1,2,0:T(1,128)}, u32[]{:S(2)}) copy-start(f32[3,3,1]{1,2,0:T(1,128)} %param.7) | copy-start | bytes 112
  2.5 12.2 %collective-permute-start.8 = (bf16[1,184,256]{2,1,0:T(8,128)(2,1)S(1)}, bf16[1,184,256]{2,1,0:T(8,128)(2,1)S(1)}, u32[]{:S(2)}, u32[]{:S(2)}) collective-permute-start(bf16[1,184,256]{2,1,0:T(8,128)(2,1)S(1)} %get-tuple-element.6.refs_4_), channel_id=1, source_target_pairs={{0,24},{1,25},{2,26},{3,27},{4,28},{5,29},{6,30},{7,31},{8,16},{9,... | collective-permute-start | bytes 282632 | tf_op jit(solution)/shard_map/ppermute | solution.py:213
  7.6 8.6 %collective-permute-start.6 = (bf16[1,184,256]{2,1,0:T(8,128)(2,1)S(1)}, bf16[1,184,256]{2,1,0:T(8,128)(2,1)S(1)}, u32[]{:S(2)}, u32[]{:S(2)}) collective-permute-start(bf16[1,184,256]{2,1,0:T(8,128)(2,1)S(1)} %get-tuple-element.6.refs_4_), channel_id=1, source_target_pairs={{0,16},{1,17},{2,18},{3,19},{4,20},{5,21},{6,22},{7,23},{8,24},{9,... | collective-permute-start | bytes 282632 | tf_op jit(solution)/shard_map/ppermute | solution.py:213
  7.6 10.0 %collective-permute-start.2 = (bf16[1,360,256]{2,1,0:T(8,128)(2,1)S(1)}, bf16[1,360,256]{2,1,0:T(8,128)(2,1)S(1)}, u32[]{:S(2)}, u32[]{:S(2)}) collective-permute-start(bf16[1,360,256]{2,1,0:T(8,128)(2,1)S(1)} %copy-done.1), channel_id=1, source_target_pairs={{0,5},{1,4},{2,7},{3,6},{4,1},{5,0},{6,3},{7,2},{8,13},{9,12},{10,... | collective-permute-start | bytes 552968 | tf_op jit(solution)/shard_map/ppermute | solution.py:213
  10.1 4.6 %collective-permute-start.10 = (s32[1,128]{1,0:T(1,128)S(1)}, s32[1,128]{1,0:T(1,128)S(1)}, u32[]{:S(2)}, u32[]{:S(2)}) collective-permute-start(s32[1,128]{1,0:T(1,128)S(1)} %get-tuple-element.7.refs_12_), channel_id=1, source_target_pairs={{0,4},{1,5},{2,6},{3,7},{4,0},{5,1},{6,2},{7,3},{8,12},{9,13},{10,... | collective-permute-start | bytes 1544 | tf_op jit(solution)/shard_map/ppermute | solution.py:213
  10.6 6.5 %collective-permute-start.4 = (bf16[1,184,256]{2,1,0:T(8,128)(2,1)S(1)}, bf16[1,184,256]{2,1,0:T(8,128)(2,1)S(1)}, u32[]{:S(2)}, u32[]{:S(2)}) collective-permute-start(bf16[1,184,256]{2,1,0:T(8,128)(2,1)S(1)} %get-tuple-element.6.refs_4_), channel_id=1, source_target_pairs={{0,8},{1,9},{2,10},{3,11},{4,12},{5,13},{6,14},{7,15},{8,0},{9,1},... | collective-permute-start | bytes 282632 | tf_op jit(solution)/shard_map/ppermute | solution.py:213
  14.7 2.5 %collective-permute-start.3 = (bf16[1,184,256]{2,1,0:T(8,128)(2,1)S(1)}, bf16[1,184,256]{2,1,0:T(8,128)(2,1)S(1)}, u32[]{:S(2)}, u32[]{:S(2)}) collective-permute-start(bf16[1,184,256]{2,1,0:T(8,128)(2,1)S(1)} %get-tuple-element.6.refs_4_), channel_id=1, source_target_pairs={{0,2},{1,3},{2,0},{3,1},{4,6},{5,7},{6,4},{7,5},{8,10},{9,11},{10,... | collective-permute-start | bytes 282632 | tf_op jit(solution)/shard_map/ppermute | solution.py:213
  14.7 7.1 %collective-permute-start.1 = (bf16[1,360,256]{2,1,0:T(8,128)(2,1)S(1)}, bf16[1,360,256]{2,1,0:T(8,128)(2,1)S(1)}, u32[]{:S(2)}, u32[]{:S(2)}) collective-permute-start(bf16[1,360,256]{2,1,0:T(8,128)(2,1)S(1)} %copy-done.1), channel_id=1, source_target_pairs={{0,4},{1,5},{2,6},{3,7},{4,0},{5,1},{6,2},{7,3},{8,12},{9,13},{10,... | collective-permute-start | bytes 552968 | tf_op jit(solution)/shard_map/ppermute | solution.py:213
  16.2 6.8 %collective-permute-start = (bf16[1,360,256]{2,1,0:T(8,128)(2,1)S(1)}, bf16[1,360,256]{2,1,0:T(8,128)(2,1)S(1)}, u32[]{:S(2)}, u32[]{:S(2)}) collective-permute-start(bf16[1,360,256]{2,1,0:T(8,128)(2,1)S(1)} %copy-done.1), channel_id=1, source_target_pairs={{0,1},{1,0},{2,3},{3,2},{4,5},{5,4},{6,7},{7,6},{8,9},{9,8},{10,11... | collective-permute-start | bytes 552968 | tf_op jit(solution)/shard_map/ppermute | solution.py:213
  17.1 5.8 %collective-permute-start.9 = (bf16[1,184,256]{2,1,0:T(8,128)(2,1)S(1)}, bf16[1,184,256]{2,1,0:T(8,128)(2,1)S(1)}, u32[]{:S(2)}, u32[]{:S(2)}) collective-permute-start(bf16[1,184,256]{2,1,0:T(8,128)(2,1)S(1)} %collective-permute-done.8.refs_10_), channel_id=1, source_target_pairs={{0,2},{1,3},{2,0},{3,1},{4,6},{5,7},{6,4},{7,5},{8,10},{9,11},{10,... | collective-permute-start | bytes 282632 | tf_op jit(solution)/shard_map/ppermute | solution.py:213
  17.1 5.8 %collective-permute-start.7 = (bf16[1,184,256]{2,1,0:T(8,128)(2,1)S(1)}, bf16[1,184,256]{2,1,0:T(8,128)(2,1)S(1)}, u32[]{:S(2)}, u32[]{:S(2)}) collective-permute-start(bf16[1,184,256]{2,1,0:T(8,128)(2,1)S(1)} %collective-permute-done.6.refs_8_), channel_id=1, source_target_pairs={{0,2},{1,3},{2,0},{3,1},{4,6},{5,7},{6,4},{7,5},{8,10},{9,11},{10,... | collective-permute-start | bytes 282632 | tf_op jit(solution)/shard_map/ppermute | solution.py:213
  17.7 5.3 %collective-permute-start.5 = (bf16[1,184,256]{2,1,0:T(8,128)(2,1)S(1)}, bf16[1,184,256]{2,1,0:T(8,128)(2,1)S(1)}, u32[]{:S(2)}, u32[]{:S(2)}) collective-permute-start(bf16[1,184,256]{2,1,0:T(8,128)(2,1)S(1)} %collective-permute-done.4.refs_6_), channel_id=1, source_target_pairs={{0,2},{1,3},{2,0},{3,1},{4,6},{5,7},{6,4},{7,5},{8,10},{9,11},{10,... | collective-permute-start | bytes 282632 | tf_op jit(solution)/shard_map/ppermute | solution.py:213
where the time goes:
time: 38.8 us; the launch traced here: 38.6 us
  starting transfers between devices  11.9 us (31%)
  blocking collectives  10 us (26%)
  waiting for transfers between devices  8.54 us (22%)
  Pallas kernels  5.8 us (15%)
  local copies, waits for them, and re-layouts  1.61 us (4%)
  between operations  0.69 us (2%)
    ppermute x11, starting transfers between devices, swap(): lax.ppermute(value, axes, [(n, n ^ distance) for n in range(plan.count)])  11.9 us
    all_to_all x1, blocking collectives, scored(): gathered = lax.all_to_all(message, axes, 0, 0, tiled=True)  10 us
    ppermute x11, waiting for transfers between devices, swap(): lax.ppermute(value, axes, [(n, n ^ distance) for n in range(plan.count)])  8.54 us
    pallas_call x1, Pallas kernels, scored(): pl.pallas_call(functools.partial(score_kernel, plan, rays, half), out_sha...  3.37 us
    pallas_call x1, Pallas kernels, scored(): pl.pallas_call(functools.partial(power_kernel, plan, rays), out_shape=(ja...  2.24 us
    unnamed x10, local copies, waits for them, and re-layouts  1.61 us
  transfers between devices with their start and end apart: 11, of which 3 were waited for; matrix products, arithmetic and copies ran while one was open for 0% of the time, Pallas kernels for 0%

commit v1 on v0

--- a/solution.py
+++ b/solution.py
@@ -10,6 +10,9 @@
 
 ITERS = 3
 LANES = 128
+TABLE = 8
+CHUNK = 256
+GROUP = 8
 SCORE_VMEM = 24 << 20
 POWER_VMEM = 16 << 20
 PAIR = 2
@@ -24,7 +27,7 @@
         self.seconds = PAIR * self.depth
         self.pairs = self.firsts * self.seconds
         self.width = -(-(3 * self.pairs + 9) // LANES) * LANES
-        self.table = -(-2 * self.rows * self.cols // LANES) * LANES
+        self.index = -(-self.pairs // LANES) * LANES
 
     def flat(self, z, x, core, c):
         return ((z * PAIR + x) * PAIR + core) * self.cols + c
@@ -35,74 +38,189 @@
     return row // (PAIR * PAIR), (row // PAIR) % PAIR, row % PAIR, c
 
 
-def prepare_kernel(plan, half, rays_ref, first_ref, second_ref, half_ref, table_ref, sem):
-    copy = pltpu.make_async_copy(rays_ref.at[:, pl.ds(0, half)], half_ref, sem)
+def prepare_kernel(
+    plan, rays_ref, first_ref, second_ref, start_ref, full_ref, half_ref, frame_ref, first_row, second_row, sems
+):
+    rays, depth = rays_ref.shape[1:]
+    half = half_ref.shape[1]
+    moves = (
+        (rays_ref.at[:, pl.ds(0, half)], half_ref),
+        (rays_ref.at[:, pl.ds(0, half)], full_ref.at[:, pl.ds(0, half)]),
+        (rays_ref.at[:, pl.ds(half, rays - half)], full_ref.at[:, pl.ds(half, rays - half)]),
+        (first_ref, first_row),
+        (second_ref, second_row),
+        (start_ref, frame_ref),
+    )
+    copies = [pltpu.make_async_copy(*move, sems.at[k]) for k, move in enumerate(moves)]
+    for copy in copies:
+        copy.start()
+    for copy in copies:
+        copy.wait()
+
+    def row(table_ref):
+        parts = [table_ref[c] for c in range(plan.cols)]
+        spare = depth - plan.rows * plan.cols
+        return jnp.concatenate(parts + [jnp.zeros((1, spare), jnp.int32)] * (spare > 0), axis=1)
+
+    first, second = row(first_row), row(second_row)
+    rows = jnp.concatenate([first >> 1, first & 1, second, jnp.zeros((TABLE - 3, depth), jnp.int32)], axis=0)
+    full_ref[0, rays : rays + TABLE] = rows.astype(jnp.float32).astype(full_ref.dtype)
+
+
+def pick_lines(own_table, next_table, own_at, next_at):
+    chosen = 0.0
+    for table, at in ((own_table, own_at), (next_table, next_at)):
+        column = lax.broadcasted_iota(jnp.int32, (table.shape[1], at.shape[1]), 0)
+        here = jnp.where(column == at, 1.0, 0.0).astype(table.dtype)
+        chosen = chosen + jnp.dot(table, here, preferred_element_type=jnp.float32)
+    return 2.0 * chosen[0:1] + chosen[1:2], chosen[2:3]
+
+
+def lines(plan, own_table, next_table):
+    z, x, core, c = position()
+    number = lax.broadcasted_iota(jnp.int32, (1, plan.pairs), 1)
+    dk, rest = number % PAIR, number // PAIR
+    dz, rest = rest % plan.depth, rest // plan.depth
+    dc, dx = rest % plan.cols, rest // plan.cols
+    at = (c ^ dc) * plan.rows + ((z ^ dz) * PAIR + x) * PAIR + (core ^ dk)
+    paired = pick_lines(own_table, next_table, jnp.where(dx == 0, at, -1), jnp.where(dx == 0, -1, at))
+    at = dc * plan.rows + (dz * PAIR + x) * PAIR + dk
+    sent = pick_lines(own_table, next_table, jnp.where(dx == x, at, -1), jnp.where(dx == x, -1, at))
+    return paired, sent
+
+
+def load_firsts(refs, stack, rows):
+    sums = []
+    for n, ref in enumerate(refs):
+        stack[n, : ref.shape[1]] = ref[0]
+        values = ref[0, : rows.shape[1]].astype(jnp.float32)
+        rows[n] = values
+        sums.append(jnp.sum(values, axis=0, keepdims=True))
+    return sums
+
+
+def load_seconds(refs, half, stack, rows):
+    sums = []
+    for m, ref in enumerate(refs):
+        stack[m, : ref.shape[1]] = ref[0]
+        values = ref[0, :half].astype(jnp.float32)
+        rows[m] = values
+        sums.append(jnp.sum(values, axis=0, keepdims=True))
+    return sums
+
+
+def cross(rays, half, firsts, seconds, first_sums, second_sums, means, parts):
+    count, first_height, depth = firsts.shape
+    second_count, second_height, _ = seconds.shape
+    scale = 1.0 / (rays * half)
+    second_sum = jnp.concatenate(second_sums, axis=0)
+    centers = []
+    for n in range(count):
+        center = jnp.sum(second_sum * first_sums[n], axis=1, keepdims=True) * scale
+        means[:second_count, n * first_height : (n + 1) * first_height] = jnp.broadcast_to(
+            center, (second_count, first_height)
+        )
+        centers.append(center)
+    total = count * first_height
+    for begin in range(0, total, CHUNK):
+        end = min(begin + CHUNK, total)
+        wanted = firsts[...].reshape(total, depth)[begin:end]
+        for low in range(0, second_count, GROUP):
+            size = min(GROUP, second_count - low)
+            corr = lax.dot_general(
+                seconds[low : low + size].reshape(size * second_height, depth),
+                wanted,
+                (((1,), (1,)), ((), ())),
+                preferred_element_type=jnp.float32,
+            )
+            for m in range(low, low + size):
+                values = corr[(m - low) * second_height : (m - low) * second_height + half]
+                top = jnp.maximum(values, means[m : m + 1, begin:end])
+                parts[m : m + 1, begin:end] = jnp.sum(top, axis=0, keepdims=True)
+    spreads = []
+    for n in range(count):
+        part = parts[:second_count, n * first_height : n * first_height + rays] - half * centers[n]
+        spreads.append(jnp.sum(part, axis=1, keepdims=True) * (2.0 * scale))
+    return centers, spreads
+
+
+def place(plan, ns, ms, centers, spreads, first_rows, second_rows, index, picked_first, picked_second):
+    z, x, core, c = position()
+    slot = (((x * plan.cols + c) * plan.depth) + z) * PAIR + core
+    wide = (len(ms), plan.width)
+    row = lax.broadcasted_iota(jnp.int32, wide, 0)
+    second = jnp.zeros(wide, jnp.int32)
+    for m, name in enumerate(ms):
+        second = jnp.where(row == m, name, second)
+    lane = lax.broadcasted_iota(jnp.int32, wide, 1)
+    placed = jnp.zeros(wide, jnp.float32)
+    for n, name in enumerate(ns):
+        for m in range(len(ms)):
+            which = name * plan.seconds + ms[m]
+            picked_first[m : m + 1, :] = first_rows[n, pl.ds(index[0, which], 1), :]
+            picked_second[m : m + 1, :] = second_rows[m, pl.ds(index[1, which], 1), :]
+        picked = jnp.sum(picked_first[: len(ms)] * picked_second[: len(ms)], axis=1, keepdims=True)
+        score = (picked - centers[n]) / (spreads[n] + 1e-05)
+        placed = placed + jnp.where(lane == slot ^ (name * plan.seconds + second), score, 0.0)
+    return jnp.sum(placed, axis=0, keepdims=True)
+
+
+def early_kernel(rays, half, ns, ms, *refs):
+    firsts, refs = refs[: len(ns)], refs[len(ns) :]
+    seconds, refs = refs[: len(ms)], refs[len(ms) :]
+    first_stack, first_rows, first_sum, second_stack, second_rows, second_sum, stats, means, parts = refs
+    first_sums = load_firsts(firsts, first_stack, first_rows)
+    second_sums = load_seconds(seconds, half, second_stack, second_rows)
+    first_sum[...] = jnp.concatenate(first_sums, axis=0)
+    second_sum[...] = jnp.concatenate(second_sums, axis=0)
+    centers, spreads = cross(rays, half, first_stack, second_stack, first_sums, second_sums, means, parts)
+    for n in range(len(ns)):
+        stats[0, n] = jnp.broadcast_to(centers[n], (len(ms), LANES))
+        stats[1, n] = jnp.broadcast_to(spreads[n], (len(ms), LANES))
+
+
+def last_kernel(plan, rays, half, early, late, *refs):
+    ns, ms = late
+    firsts, refs = refs[: len(ns)], refs[len(ns) :]
+    seconds, refs = refs[: len(ms)], refs[len(ms) :]
+    early_firsts, early_rows, early_sum, early_seconds, early_second_rows, early_second_sum = refs[:6]
+    early_stats, own_ref, start_ref, message_ref, index_row, index, sem = refs[6:13]
+    first_stack, first_rows, second_stack, second_rows, means, parts, picked_first, picked_second = refs[13:]
+    own_table = own_ref[0, rays : rays + TABLE]
+    next_table = firsts[ns.index(plan.cols)][0, rays : rays + TABLE]
+    paired, sent = lines(plan, own_table, next_table)
+    index_row[0:1, : plan.pairs] = paired[0].astype(jnp.int32)
+    index_row[1:2, : plan.pairs] = paired[1].astype(jnp.int32)
+    copy = pltpu.make_async_copy(index_row, index, sem)
     copy.start()
-    parts = [first_ref[c] for c in range(plan.cols)] + [second_ref[c] for c in range(plan.cols)]
-    spare = plan.table - 2 * plan.rows * plan.cols
-    if spare:
-        parts.append(jnp.zeros((1, spare), jnp.int32))
-    table_ref[...] = jnp.concatenate(parts, axis=1)
+    first_sums = load_firsts(firsts, first_stack, first_rows)
+    second_sums = load_seconds(seconds, half, second_stack, second_rows)
+    old_first_sums = [early_sum[n : n + 1] for n in range(len(early[0]))]
+    old_second_sums = [early_second_sum[m : m + 1] for m in range(len(early[1]))]
+    blocks = (
+        (ns, early[1], first_rows, early_second_rows),
+        (early[0], ms, early_rows, second_rows),
+        (ns, ms, first_rows, second_rows),
+        (early[0], early[1], early_rows, early_second_rows),
+    )
+    arrays = (
+        (first_stack, early_seconds, first_sums, old_second_sums),
+        (early_firsts, second_stack, old_first_sums, second_sums),
+        (first_stack, second_stack, first_sums, second_sums),
+    )
+    stats = [cross(rays, half, *arrays[k], means.at[k], parts.at[k]) for k in range(3)]
+    stats.append([[early_stats[kind, n][:, 0:1] for n in range(len(early[0]))] for kind in range(2)])
     copy.wait()
-
-
-def score_kernel(plan, rays, half, *refs):
-    fulls = refs[: plan.firsts]
-    halves = refs[plan.firsts : plan.firsts + plan.seconds]
-    own_table, next_table, start_ref, message_ref = refs[plan.firsts + plan.seconds : -6]
-    full_rows, half_rows, first_rows, second_rows, parts, means = refs[-6:]
-    z, x, core, c = position()
-    scale = 1.0 / (rays * half)
-
-    full_sums, half_sums = [], []
-    for n, ref in enumerate(fulls):
-        values = ref[0].astype(jnp.float32)
-        full_rows[n] = values
-        full_sums.append(jnp.sum(values, axis=0, keepdims=True))
-    for n, ref in enumerate(halves):
-        values = ref[0, :half].astype(jnp.float32)
-        half_rows[n] = values
-        half_sums.append(jnp.sum(values, axis=0, keepdims=True))
-    half_sum = jnp.concatenate(half_sums, axis=0)
-    for n in range(plan.firsts):
-        means[pl.ds(n * plan.seconds, plan.seconds), :] = jnp.broadcast_to(
-            jnp.sum(half_sum * full_sums[n], axis=1, keepdims=True) * scale, (plan.seconds, LANES)
+    spare = plan.width - 3 * plan.pairs - 9
+    message = jnp.concatenate(
+        [jnp.zeros((1, plan.pairs), jnp.float32), *sent, *(start_ref[k] for k in range(3))]
+        + [jnp.zeros((1, spare), jnp.float32)] * (spare > 0),
+        axis=1,
+    )
+    for k, (one, two, one_rows, two_rows) in enumerate(blocks):
+        message = message + place(
+            plan, one, two, *stats[k], one_rows, two_rows, index, picked_first.at[k], picked_second.at[k]
         )
-
-    lane = lax.broadcasted_iota(jnp.int32, (1, plan.width), 1)
-    lines = jnp.zeros((1, plan.width), jnp.int32)
-    own_slot = (((x * plan.cols + c) * plan.depth) + z) * PAIR + core
-    for n in range(plan.firsts):
-        dx, dc = n // plan.cols, n % plan.cols
-        table = next_table if dx else own_table
-        for m in range(plan.seconds):
-            dz, dk = m // PAIR, m % PAIR
-            pair = n * plan.seconds + m
-            at = (c ^ dc) * plan.rows + ((z ^ dz) * PAIR + x) * PAIR + (core ^ dk)
-            a = table[0, at]
-            b = table[0, plan.rows * plan.cols + at]
-            first_rows[pl.ds(pair, 1), :] = full_rows[n, pl.ds(a, 1), :]
-            second_rows[pl.ds(pair, 1), :] = half_rows[m, pl.ds(b, 1), :]
-            slot = own_slot ^ pair
-            lines = jnp.where(lane == plan.pairs + slot, a, lines)
-            lines = jnp.where(lane == 2 * plan.pairs + slot, b, lines)
-            corr = lax.dot_general(
-                halves[m][0, :half], fulls[n][0], (((1,), (1,)), ((), ())), preferred_element_type=jnp.float32
-            )
-            center = means[pl.ds(pair, 1), 0:1]
-            parts[pl.ds(pair, 1), :] = jnp.sum(jnp.abs(corr - center), axis=0, keepdims=True)
-
-    center = means[:, 0:1]
-    spread = jnp.sum(parts[...], axis=1, keepdims=True) * scale
-    picked = jnp.sum(first_rows[...] * second_rows[...], axis=1, keepdims=True)
-    score = (picked - center) / (spread + 1e-05)
-    wide = (plan.pairs, plan.width)
-    to = own_slot ^ lax.broadcasted_iota(jnp.int32, wide, 0)
-    here = lax.broadcasted_iota(jnp.int32, wide, 1) == to
-    message = jnp.sum(jnp.where(here, score, 0.0), axis=0, keepdims=True) + lines.astype(jnp.float32)
-    for k in range(3):
-        for q in range(3):
-            message = jnp.where(lane == 3 * plan.pairs + 3 * k + q, start_ref[k, 0, q], message)
     message_ref[...] = jnp.broadcast_to(message[None], message_ref.shape)
 
 
@@ -206,52 +324,80 @@
     half_tiled = -(-half // 8) * 8
     axes = ("row", "col")
     vmem = pl.BlockSpec(memory_space=pltpu.VMEM)
-    smem = pl.BlockSpec(memory_space=pltpu.SMEM)
-    anywhere = pl.BlockSpec(memory_space=pl.ANY)
 
     def swap(value, distance):
         return lax.ppermute(value, axes, [(n, n ^ distance) for n in range(plan.count)])
 
     first = jnp.transpose(first_line, (0, 2, 1))
     second = jnp.transpose(second_line, (0, 2, 1))
-    half_rays, own_table = pl.pallas_call(
-        functools.partial(prepare_kernel, plan, half_tiled),
+    start = jnp.transpose(start_frame, (0, 2, 1))
+    inputs = [pltpu.with_memory_space_constraint(one, pltpu.HBM) for one in (polar_rays, first, second, start)]
+    own_rays, half_rays, own_frame = pl.pallas_call(
+        functools.partial(prepare_kernel, plan),
         out_shape=(
+            jax.ShapeDtypeStruct((1, rays + TABLE, depth), polar_rays.dtype),
             jax.ShapeDtypeStruct((1, half_tiled, depth), polar_rays.dtype),
-            jax.ShapeDtypeStruct((1, plan.table), jnp.int32),
+            jax.ShapeDtypeStruct(start.shape, start.dtype),
         ),
-        in_specs=[anywhere, vmem, vmem],
-        out_specs=(vmem, vmem),
-        scratch_shapes=[pltpu.SemaphoreType.DMA],
+        in_specs=[pl.BlockSpec(memory_space=pltpu.HBM)] * 4,
+        out_specs=(vmem, vmem, vmem),
+        scratch_shapes=[
+            pltpu.VMEM(first.shape, first.dtype),
+            pltpu.VMEM(second.shape, second.dtype),
+            pltpu.SemaphoreType.DMA((6,)),
+        ],
         compiler_params=pltpu.CompilerParams(vmem_limit_bytes=1 << 20),
         name="prepare",
-    )(polar_rays, first, second)
-
-    next_table = swap(own_table, plan.flat(0, 1, 0, 0))
-    fulls = [polar_rays] + [
-        swap(polar_rays, plan.flat(0, n // plan.cols, 0, n % plan.cols)) for n in range(1, plan.firsts)
-    ]
+    )(*inputs)
+    fulls = [own_rays] + [swap(own_rays, plan.flat(0, n // plan.cols, 0, n % plan.cols)) for n in range(1, plan.firsts)]
     deep = [half_rays] + [swap(half_rays, plan.flat(dz, 0, 0, 0)) for dz in range(1, plan.depth)]
     halves = []
     for piece in deep:
         halves += [piece, swap(piece, plan.flat(0, 0, 1, 0))]
 
+    first_height, second_height = -(-rays // 16) * 16, -(-half // 16) * 16
+    params = pltpu.CompilerParams(vmem_limit_bytes=SCORE_VMEM)
+    (early_ns, early_ms), (late_ns, late_ms) = early_part(plan), late_part(plan)
+
+    def stacks(ns, ms):
+        return [
+            ((len(ns), first_height, depth), polar_rays.dtype),
+            ((len(ns), rays, depth), jnp.float32),
+            ((len(ns), depth), jnp.float32),
+            ((len(ms), second_height, depth), polar_rays.dtype),
+            ((len(ms), half, depth), jnp.float32),
+            ((len(ms), depth), jnp.float32),
+        ]
+
+    most = max(len(early_ms), len(late_ms))
+    span = max(len(early_ns), len(late_ns)) * first_height
+    before = pl.pallas_call(
+        functools.partial(early_kernel, rays, half, early_ns, early_ms),
+        out_shape=[jax.ShapeDtypeStruct(*one) for one in stacks(early_ns, early_ms)]
+        + [jax.ShapeDtypeStruct((2, len(early_ns), len(early_ms), LANES), jnp.float32)],
+        in_specs=[vmem] * (len(early_ns) + len(early_ms)),
+        out_specs=[vmem] * 7,
+        compiler_params=params,
+        scratch_shapes=[pltpu.VMEM((most, span), jnp.float32)] * 2,
+        name="early",
+    )(*(fulls[n] for n in early_ns), *(halves[m] for m in early_ms))
+    new = stacks(late_ns, late_ms)
     message = pl.pallas_call(
-        functools.partial(score_kernel, plan, rays, half),
+        functools.partial(last_kernel, plan, rays, half, (early_ns, early_ms), (late_ns, late_ms)),
         out_shape=jax.ShapeDtypeStruct((plan.count, 1, plan.width), jnp.float32),
-        in_specs=[vmem] * (plan.firsts + plan.seconds) + [smem, smem, smem],
+        in_specs=[vmem] * (len(late_ns) + len(late_ms) + 9),
         out_specs=vmem,
-        compiler_params=pltpu.CompilerParams(vmem_limit_bytes=SCORE_VMEM),
+        compiler_params=params,
         scratch_shapes=[
-            pltpu.VMEM((plan.firsts, rays, depth), jnp.float32),
-            pltpu.VMEM((plan.seconds, half, depth), jnp.float32),
-            pltpu.VMEM((plan.pairs, depth), jnp.float32),
-            pltpu.VMEM((plan.pairs, depth), jnp.float32),
-            pltpu.VMEM((plan.pairs, rays), jnp.float32),
-            pltpu.VMEM((plan.pairs, LANES), jnp.float32),
-        ],
-        name="score",
-    )(*fulls, *halves, own_table, next_table, jnp.transpose(start_frame, (0, 2, 1)))
+            pltpu.VMEM((2, plan.index), jnp.int32),
+            pltpu.SMEM((2, plan.index), jnp.int32),
+            pltpu.SemaphoreType.DMA,
+        ]
+        + [pltpu.VMEM(*one) for one in (new[0], new[1], new[3], new[4])]
+        + [pltpu.VMEM((3, most, span), jnp.float32)] * 2
+        + [pltpu.VMEM((4, most, depth), jnp.float32)] * 2,
+        name="last",
+    )(*(fulls[n] for n in late_ns), *(halves[m] for m in late_ms), *before, own_rays, own_frame)
 
     gathered = lax.all_to_all(message, axes, 0, 0, tiled=True)
 
@@ -278,6 +424,19 @@
     return scored(plan, *arrays)
 
 
+def early_part(plan):
+    deep = [0] + list(range(plan.depth - 1, plan.depth // 2, -1))
+    return (0, plan.firsts - 1), tuple(PAIR * dz + dk for dz in deep for dk in range(PAIR))
+
+
+def late_part(plan):
+    ns, ms = early_part(plan)
+    return (
+        tuple(n for n in range(plan.firsts) if n not in ns),
+        tuple(m for m in range(plan.seconds) if m not in ms),
+    )
+
+
 def solution(mesh):
     plan = Plan(mesh.shape["row"], mesh.shape["col"])
     placed = (

time: 38.8 us -> 36.2 us (0.933)
  waiting for transfers between devices: 8.54 us -> 5.48 us
  blocking collectives: 10 us -> 12.1 us
  local copies, waits for them, and re-layouts: 1.61 us -> 0 us
    ppermute x11 -> x10, waiting for transfers between devices: 8.54 us -> 5.48 us  [swap(): lax.ppermute(value, axes, [(n, n ^ distance) for n in range(plan.count)])]
    all_to_all x1, blocking collectives: 10 us -> 12.1 us  [scored(): gathered = lax.all_to_all(message, axes, 0, 0, tiled=True)]
    unnamed x10 -> x0, local copies, waits for them, and re-layouts: 1.61 us -> none
    pallas_call x2 -> x3, Pallas kernels: 3.55 us -> 3.52 us  [the longest x1 1.64 us: scored(): pl.pallas_call(functools.partial(last_kernel, plan, rays, half, (early_ns...]
    ppermute x11 -> x10, starting transfers between devices: 11.9 us -> 12 us  [swap(): lax.ppermute(value, axes, [(n, n ^ distance) for n in range(plan.count)])]
  transfers between devices with their start and end apart: 11 -> 10, of which waited for: 3 -> 5; matrix products, arithmetic and copies ran while one was open for 0% -> 0% of each run, Pallas kernels for 0% -> 2%
where the time goes in v1:
time: 36.2 us; the launch traced here: 36 us
  blocking collectives  12.1 us (33%)
  starting transfers between devices  12 us (33%)
  Pallas kernels  5.76 us (16%)
  waiting for transfers between devices  5.48 us (15%)
  between operations  0.66 us (2%)
    all_to_all x1, blocking collectives, scored(): gathered = lax.all_to_all(message, axes, 0, 0, tiled=True)  12.1 us
    ppermute x10, starting transfers between devices, swap(): lax.ppermute(value, axes, [(n, n ^ distance) for n in range(plan.count)])  12 us
    ppermute x10, waiting for transfers between devices, swap(): lax.ppermute(value, axes, [(n, n ^ distance) for n in range(plan.count)])  5.48 us
    pallas_call x1, Pallas kernels, scored(): pl.pallas_call(functools.partial(power_kernel, plan, rays), out_shape=(ja...  2.24 us
    pallas_call x1, Pallas kernels, scored(): pl.pallas_call(functools.partial(last_kernel, plan, rays, half, (early_ns...  1.64 us
    pallas_call x1, Pallas kernels, scored(): pl.pallas_call(functools.partial(prepare_kernel, plan), out_shape=(jax.Sh...  1.12 us
    pallas_call x1, Pallas kernels, scored(): pl.pallas_call(functools.partial(early_kernel, rays, half, early_ns, earl...  0.76 us
  transfers between devices with their start and end apart: 10, of which 5 were waited for; matrix products, arithmetic and copies ran while one was open for 0% of the time, Pallas kernels for 2%

profile of v1, /device:TPU:0, one launch (start us, length us, event | category | flops | bytes accessed | tf_op | source)
XLA Modules:
  0.0 36.0 jit_solution(14986183148254473362)
XLA Ops:
  0.6 1.1 %prepare.1 = (bf16[1,368,256]{2,1,0:T(8,128)(2,1)S(1)}, bf16[1,184,256]{2,1,0:T(8,128)(2,1)S(1)}, f32[3,1,3]{2,1,0:T(1,128)S(1)}) custom-call(bf16[1,360,256]{2,1,0:T(8,128)(2,1)} %rays_ref.1, s32[2,1,16]{2,1,0:T(1,128)} %bitcast.12, s32[2,1,16]{2,1,0:T(1,128)} %bitcast.13, f32[3,1,3]{2,1,0:T(1,128)} %bitcast.11), custom_call_target="tpu_custom_call" | custom-call | tf_op jit(solution)/shard_map/prepare/pallas_call | solution.py:335
  1.8 5.1 %collective-permute-start.8 = (bf16[1,184,256]{2,1,0:T(8,128)(2,1)S(1)}, bf16[1,184,256]{2,1,0:T(8,128)(2,1)S(1)}, u32[]{:S(2)}, u32[]{:S(2)}) collective-permute-start(bf16[1,184,256]{2,1,0:T(8,128)(2,1)S(1)} %get-tuple-element.15.refs_2_), channel_id=1, source_target_pairs={{0,24},{1,25},{2,26},{3,27},{4,28},{5,29},{6,30},{7,31},{8,16},{9,... | collective-permute-start | bytes 282632 | tf_op jit(solution)/shard_map/ppermute | solution.py:329
  6.9 0.0 collective-permute-start.7
  6.9 0.0 collective-permute-start.2
  6.9 0.7 %collective-permute-start.4 = (bf16[1,184,256]{2,1,0:T(8,128)(2,1)S(1)}, bf16[1,184,256]{2,1,0:T(8,128)(2,1)S(1)}, u32[]{:S(2)}, u32[]{:S(2)}) collective-permute-start(bf16[1,184,256]{2,1,0:T(8,128)(2,1)S(1)} %get-tuple-element.15.refs_2_), channel_id=1, source_target_pairs={{0,16},{1,17},{2,18},{3,19},{4,20},{5,21},{6,22},{7,23},{8,24},{9,... | collective-permute-start | bytes 282632 | tf_op jit(solution)/shard_map/ppermute | solution.py:329
  7.6 2.5 %collective-permute-start.6 = (bf16[1,368,256]{2,1,0:T(8,128)(2,1)S(1)}, bf16[1,368,256]{2,1,0:T(8,128)(2,1)S(1)}, u32[]{:S(2)}, u32[]{:S(2)}) collective-permute-start(bf16[1,368,256]{2,1,0:T(8,128)(2,1)S(1)} %get-tuple-element.14.refs_0_.refs_13_), channel_id=1, source_target_pairs={{0,5},{1,4},{2,7},{3,6},{4,1},{5,0},{6,3},{7,2},{8,13},{9,12},{10,... | collective-permute-start | bytes 565256 | tf_op jit(solution)/shard_map/ppermute | solution.py:329
  10.1 0.3 collective-permute-done.8.refs_4_
  10.4 0.0 collective-permute-start.9
  10.4 0.0 collective-permute-done.7.refs_3_
  10.4 1.6 %collective-permute-start = (bf16[1,368,256]{2,1,0:T(8,128)(2,1)S(1)}, bf16[1,368,256]{2,1,0:T(8,128)(2,1)S(1)}, u32[]{:S(2)}, u32[]{:S(2)}) collective-permute-start(bf16[1,368,256]{2,1,0:T(8,128)(2,1)S(1)} %get-tuple-element.14.refs_0_.refs_13_), channel_id=1, source_target_pairs={{0,1},{1,0},{2,3},{3,2},{4,5},{5,4},{6,7},{7,6},{8,9},{9,8},{10,11... | collective-permute-start | bytes 565256 | tf_op jit(solution)/shard_map/ppermute | solution.py:329
  12.0 1.5 %collective-permute-done.2.refs_2_ = bf16[1,184,256]{2,1,0:T(8,128)(2,1)S(1)} collective-permute-done((bf16[1,184,256]{2,1,0:T(8,128)(2,1)S(1)}, bf16[1,184,256]{2,1,0:T(8,128)(2,1)S(1)}, u32[]{:S(2)}, u32[]{:S(2)}) %collective-permute-start.2) | collective-permute-done | bytes 94240 | tf_op jit(solution)/shard_map/ppermute | solution.py:329
  13.5 1.5 %collective-permute-start.1 = (bf16[1,368,256]{2,1,0:T(8,128)(2,1)S(1)}, bf16[1,368,256]{2,1,0:T(8,128)(2,1)S(1)}, u32[]{:S(2)}, u32[]{:S(2)}) collective-permute-start(bf16[1,368,256]{2,1,0:T(8,128)(2,1)S(1)} %get-tuple-element.14.refs_0_.refs_13_), channel_id=1, source_target_pairs={{0,4},{1,5},{2,6},{3,7},{4,0},{5,1},{6,2},{7,3},{8,12},{9,13},{10,... | collective-permute-start | bytes 565256 | tf_op jit(solution)/shard_map/ppermute | solution.py:329
  15.0 0.0 collective-permute-done.4.refs_4_
  15.0 0.0 collective-permute-start.3
  15.0 0.0 collective-permute-done.9.refs_5_
  15.0 0.5 %collective-permute-start.5 = (bf16[1,184,256]{2,1,0:T(8,128)(2,1)S(1)}, bf16[1,184,256]{2,1,0:T(8,128)(2,1)S(1)}, u32[]{:S(2)}, u32[]{:S(2)}) collective-permute-start(bf16[1,184,256]{2,1,0:T(8,128)(2,1)S(1)} %collective-permute-done.4.refs_4_), channel_id=1, source_target_pairs={{0,2},{1,3},{2,0},{3,1},{4,6},{5,7},{6,4},{7,5},{8,10},{9,11},{10,... | collective-permute-start | bytes 282632 | tf_op jit(solution)/shard_map/ppermute | solution.py:329
  15.5 0.8 %early.1 = (bf16[2,368,256]{2,1,0:T(8,128)(2,1)S(1)}, f32[2,360,256]{2,1,0:T(8,128)S(1)}, f32[2,256]{1,0:T(2,128)S(1)}, bf16[4,192,256]{2,1,0:T(8,128)(2,1)S(1)}...) custom-call(bf16[1,368,256]{2,1,0:T(8,128)(2,1)S(1)} %get-tuple-element.14.refs_0_.refs_13_, ...), custom_call_target="tpu_custom_call" | custom-call | tf_op jit(solution)/shard_map/early/pallas_call | solution.py:374
  16.3 0.0 collective-permute-done.3.refs_3_
  16.3 0.2 collective-permute-done.5.refs_5_
  16.4 2.6 %collective-permute-done.refs_0_ = bf16[1,368,256]{2,1,0:T(8,128)(2,1)S(1)} collective-permute-done((bf16[1,368,256]{2,1,0:T(8,128)(2,1)S(1)}, bf16[1,368,256]{2,1,0:T(8,128)(2,1)S(1)}, u32[]{:S(2)}, u32[]{:S(2)}) %collective-permute-start) | collective-permute-done | bytes 188448 | tf_op jit(solution)/shard_map/ppermute | solution.py:329
  19.1 0.9 %collective-permute-done.1.refs_1_ = bf16[1,368,256]{2,1,0:T(8,128)(2,1)S(1)} collective-permute-done((bf16[1,368,256]{2,1,0:T(8,128)(2,1)S(1)}, bf16[1,368,256]{2,1,0:T(8,128)(2,1)S(1)}, u32[]{:S(2)}, u32[]{:S(2)}) %collective-permute-start.1) | collective-permute-done | bytes 188448 | tf_op jit(solution)/shard_map/ppermute | solution.py:329
  20.0 1.6 %last.1 = f32[32,1,128]{2,1,0:T(1,128)S(1)} custom-call(bf16[1,368,256]{2,1,0:T(8,128)(2,1)S(1)} %collective-permute-done.refs_0_, bf16[1,368,256]{2,1,0:T(8,128)(2,1)S(1)} %collective-permute-done.1.refs_1_, bf16[1,184,256]{2,1,0:T(8,128)(2,1)S(1)} %collective-permute-done.2.refs_2_, bf16[1,184,256]{2,1,0:T(8,128)(2,1)S(1)} %collective-permute-done.3.refs_3_, ...), custom_call_target="tpu_custom_call" | custom-call | tf_op jit(solution)/shard_map/last/pallas_call | solution.py:385
  21.6 12.1 %all_to_all.5.gathered_ref = f32[32,1,128]{2,1,0:T(1,128)S(1)} all-to-all(f32[32,1,128]{2,1,0:T(1,128)S(1)} %last.1), channel_id=1, replica_groups=mesh['row'=16,'col'=2] {'row','col'}, dimensions={0} | all-to-all | bytes 32768 | tf_op jit(solution)/shard_map/all_to_all | solution.py:402
  33.7 2.2 %power.1 = (f32[2,1,16]{2,1,0:T(1,128)}, f32[3,1,3]{2,1,0:T(1,128)}) custom-call(f32[32,1,128]{2,1,0:T(1,128)S(1)} %all_to_all.5.gathered_ref), custom_call_target="tpu_custom_call" | custom-call | tf_op jit(solution)/shard_map/power/pallas_call | solution.py:404
  (1 shorter events, 0.0 us)
Async XLA Ops:
  1.8 8.7 %collective-permute-start.8 = (bf16[1,184,256]{2,1,0:T(8,128)(2,1)S(1)}, bf16[1,184,256]{2,1,0:T(8,128)(2,1)S(1)}, u32[]{:S(2)}, u32[]{:S(2)}) collective-permute-start(bf16[1,184,256]{2,1,0:T(8,128)(2,1)S(1)} %get-tuple-element.15.refs_2_), channel_id=1, source_target_pairs={{0,24},{1,25},{2,26},{3,27},{4,28},{5,29},{6,30},{7,31},{8,16},{9,... | collective-permute-start | bytes 282632 | tf_op jit(solution)/shard_map/ppermute | solution.py:329
  6.9 3.5 %collective-permute-start.7 = (bf16[1,184,256]{2,1,0:T(8,128)(2,1)S(1)}, bf16[1,184,256]{2,1,0:T(8,128)(2,1)S(1)}, u32[]{:S(2)}, u32[]{:S(2)}) collective-permute-start(bf16[1,184,256]{2,1,0:T(8,128)(2,1)S(1)} %get-tuple-element.15.refs_2_), channel_id=1, source_target_pairs={{0,2},{1,3},{2,0},{3,1},{4,6},{5,7},{6,4},{7,5},{8,10},{9,11},{10,... | collective-permute-start | bytes 282632 | tf_op jit(solution)/shard_map/ppermute | solution.py:329
  6.9 6.6 %collective-permute-start.2 = (bf16[1,184,256]{2,1,0:T(8,128)(2,1)S(1)}, bf16[1,184,256]{2,1,0:T(8,128)(2,1)S(1)}, u32[]{:S(2)}, u32[]{:S(2)}) collective-permute-start(bf16[1,184,256]{2,1,0:T(8,128)(2,1)S(1)} %get-tuple-element.15.refs_2_), channel_id=1, source_target_pairs={{0,8},{1,9},{2,10},{3,11},{4,12},{5,13},{6,14},{7,15},{8,0},{9,1},... | collective-permute-start | bytes 282632 | tf_op jit(solution)/shard_map/ppermute | solution.py:329
  6.9 8.1 %collective-permute-start.4 = (bf16[1,184,256]{2,1,0:T(8,128)(2,1)S(1)}, bf16[1,184,256]{2,1,0:T(8,128)(2,1)S(1)}, u32[]{:S(2)}, u32[]{:S(2)}) collective-permute-start(bf16[1,184,256]{2,1,0:T(8,128)(2,1)S(1)} %get-tuple-element.15.refs_2_), channel_id=1, source_target_pairs={{0,16},{1,17},{2,18},{3,19},{4,20},{5,21},{6,22},{7,23},{8,24},{9,... | collective-permute-start | bytes 282632 | tf_op jit(solution)/shard_map/ppermute | solution.py:329
  7.6 7.9 %collective-permute-start.6 = (bf16[1,368,256]{2,1,0:T(8,128)(2,1)S(1)}, bf16[1,368,256]{2,1,0:T(8,128)(2,1)S(1)}, u32[]{:S(2)}, u32[]{:S(2)}) collective-permute-start(bf16[1,368,256]{2,1,0:T(8,128)(2,1)S(1)} %get-tuple-element.14.refs_0_.refs_13_), channel_id=1, source_target_pairs={{0,5},{1,4},{2,7},{3,6},{4,1},{5,0},{6,3},{7,2},{8,13},{9,12},{10,... | collective-permute-start | bytes 565256 | tf_op jit(solution)/shard_map/ppermute | solution.py:329
  10.4 4.6 %collective-permute-start.9 = (bf16[1,184,256]{2,1,0:T(8,128)(2,1)S(1)}, bf16[1,184,256]{2,1,0:T(8,128)(2,1)S(1)}, u32[]{:S(2)}, u32[]{:S(2)}) collective-permute-start(bf16[1,184,256]{2,1,0:T(8,128)(2,1)S(1)} %collective-permute-done.8.refs_4_), channel_id=1, source_target_pairs={{0,2},{1,3},{2,0},{3,1},{4,6},{5,7},{6,4},{7,5},{8,10},{9,11},{10,... | collective-permute-start | bytes 282632 | tf_op jit(solution)/shard_map/ppermute | solution.py:329
  10.4 8.6 %collective-permute-start = (bf16[1,368,256]{2,1,0:T(8,128)(2,1)S(1)}, bf16[1,368,256]{2,1,0:T(8,128)(2,1)S(1)}, u32[]{:S(2)}, u32[]{:S(2)}) collective-permute-start(bf16[1,368,256]{2,1,0:T(8,128)(2,1)S(1)} %get-tuple-element.14.refs_0_.refs_13_), channel_id=1, source_target_pairs={{0,1},{1,0},{2,3},{3,2},{4,5},{5,4},{6,7},{7,6},{8,9},{9,8},{10,11... | collective-permute-start | bytes 565256 | tf_op jit(solution)/shard_map/ppermute | solution.py:329
  13.5 6.5 %collective-permute-start.1 = (bf16[1,368,256]{2,1,0:T(8,128)(2,1)S(1)}, bf16[1,368,256]{2,1,0:T(8,128)(2,1)S(1)}, u32[]{:S(2)}, u32[]{:S(2)}) collective-permute-start(bf16[1,368,256]{2,1,0:T(8,128)(2,1)S(1)} %get-tuple-element.14.refs_0_.refs_13_), channel_id=1, source_target_pairs={{0,4},{1,5},{2,6},{3,7},{4,0},{5,1},{6,2},{7,3},{8,12},{9,13},{10,... | collective-permute-start | bytes 565256 | tf_op jit(solution)/shard_map/ppermute | solution.py:329
  15.0 1.3 %collective-permute-start.3 = (bf16[1,184,256]{2,1,0:T(8,128)(2,1)S(1)}, bf16[1,184,256]{2,1,0:T(8,128)(2,1)S(1)}, u32[]{:S(2)}, u32[]{:S(2)}) collective-permute-start(bf16[1,184,256]{2,1,0:T(8,128)(2,1)S(1)} %collective-permute-done.2.refs_2_), channel_id=1, source_target_pairs={{0,2},{1,3},{2,0},{3,1},{4,6},{5,7},{6,4},{7,5},{8,10},{9,11},{10,... | collective-permute-start | bytes 282632 | tf_op jit(solution)/shard_map/ppermute | solution.py:329
  15.0 1.4 %collective-permute-start.5 = (bf16[1,184,256]{2,1,0:T(8,128)(2,1)S(1)}, bf16[1,184,256]{2,1,0:T(8,128)(2,1)S(1)}, u32[]{:S(2)}, u32[]{:S(2)}) collective-permute-start(bf16[1,184,256]{2,1,0:T(8,128)(2,1)S(1)} %collective-permute-done.4.refs_4_), channel_id=1, source_target_pairs={{0,2},{1,3},{2,0},{3,1},{4,6},{5,7},{6,4},{7,5},{8,10},{9,11},{10,... | collective-permute-start | bytes 282632 | tf_op jit(solution)/shard_map/ppermute | solution.py:329

commit v2 on v1

--- a/solution.py
+++ b/solution.py
@@ -261,30 +261,38 @@
         jnp.concatenate([turned[at + 3 * k + q : at + 3 * k + q + 1] for q in range(3)], axis=1) for k in range(3)
     ]
     pad = jnp.zeros((5, 3 * count), jnp.float32)
-    for _ in range(ITERS):
-        stacked = jnp.concatenate(frames + [pad], axis=0)
+
+    def applied(values):
         mixed = lax.dot_general(
-            stacked,
+            jnp.concatenate(values + [pad], axis=0),
             matrix_ref[...],
             (((1,), (1,)), ((), ())),
             precision=lax.Precision.HIGHEST,
             preferred_element_type=jnp.float32,
         )
-        y = [mixed[k : k + 1] for k in range(3)]
-
-        def gram(k, l):
-            return jnp.sum(y[k] * y[l], axis=1, keepdims=True)
-
-        f00 = jnp.sqrt(gram(0, 0))
-        f10 = gram(1, 0) / f00
-        f20 = gram(2, 0) / f00
-        f11 = jnp.sqrt(gram(1, 1) - f10 * f10)
-        f21 = (gram(2, 1) - f20 * f10) / f11
-        f22 = jnp.sqrt(gram(2, 2) - f20 * f20 - f21 * f21)
-        v0 = y[0] / f00
-        v1 = (y[1] - f10 * v0) / f11
-        v2 = (y[2] - f20 * v0 - f21 * v1) / f22
-        frames = [v0, v1, v2]
+        return [mixed[k : k + 1] for k in range(3)]
+
+    def factor(y):
+        g00, g10, g20, g11, g21, g22 = (
+            jnp.sum(y[k] * y[l], axis=1, keepdims=True) for k, l in ((0, 0), (1, 0), (2, 0), (1, 1), (2, 1), (2, 2))
+        )
+        r0 = lax.rsqrt(g00)
+        f10, f20 = g10 * r0, g20 * r0
+        r1 = lax.rsqrt(g11 - f10 * f10)
+        f21 = (g21 - f20 * f10) * r1
+        r2 = lax.rsqrt(g22 - f20 * f20 - f21 * f21)
+        return f10, f20, f21, r0, r1, r2
+
+    def solved(parts, y):
+        f10, f20, f21, r0, r1, r2 = parts
+        v0 = y[0] * r0
+        v1 = (y[1] - f10 * v0) * r1
+        return [v0, v1, (y[2] - f20 * v0 - f21 * v1) * r2]
+
+    y = applied(frames)
+    for _ in range(ITERS - 1):
+        y = solved(factor(y), applied(y))
+    frames = solved(factor(y), y)
 
     own = (x * plan.cols + c) * seconds + z * PAIR + core
     wide = lax.broadcasted_iota(jnp.int32, (1, 3 * count), 1)

time: 36.2 us -> 35.8 us (0.989)
  Pallas kernels: 5.76 us -> 5.37 us
    pallas_call x1, Pallas kernels: 2.24 us -> 1.85 us  [scored(): pl.pallas_call(functools.partial(power_kernel, plan, rays), out_shape=(ja...]
where the time goes in v2:
time: 35.8 us; the launch traced here: 35.6 us
  blocking collectives  12.1 us (34%)
  starting transfers between devices  12 us (34%)
  waiting for transfers between devices  5.48 us (15%)
  Pallas kernels  5.37 us (15%)
  between operations  0.66 us (2%)
    all_to_all x1, blocking collectives, scored(): gathered = lax.all_to_all(message, axes, 0, 0, tiled=True)  12.1 us
    ppermute x10, starting transfers between devices, swap(): lax.ppermute(value, axes, [(n, n ^ distance) for n in range(plan.count)])  12 us
    ppermute x10, waiting for transfers between devices, swap(): lax.ppermute(value, axes, [(n, n ^ distance) for n in range(plan.count)])  5.48 us
    pallas_call x1, Pallas kernels, scored(): pl.pallas_call(functools.partial(power_kernel, plan, rays), out_shape=(ja...  1.85 us
    pallas_call x1, Pallas kernels, scored(): pl.pallas_call(functools.partial(last_kernel, plan, rays, half, (early_ns...  1.64 us
    pallas_call x1, Pallas kernels, scored(): pl.pallas_call(functools.partial(prepare_kernel, plan), out_shape=(jax.Sh...  1.12 us
    pallas_call x1, Pallas kernels, scored(): pl.pallas_call(functools.partial(early_kernel, rays, half, early_ns, earl...  0.76 us
  transfers between devices with their start and end apart: 10, of which 5 were waited for; matrix products, arithmetic and copies ran while one was open for 0% of the time, Pallas kernels for 2%

profile of v2, /device:TPU:0, one launch (start us, length us, event | category | flops | bytes accessed | tf_op | source)
XLA Modules:
  0.0 35.6 jit_solution(15321920064646502593)
XLA Ops:
  0.6 1.1 %prepare.1 = (bf16[1,368,256]{2,1,0:T(8,128)(2,1)S(1)}, bf16[1,184,256]{2,1,0:T(8,128)(2,1)S(1)}, f32[3,1,3]{2,1,0:T(1,128)S(1)}) custom-call(bf16[1,360,256]{2,1,0:T(8,128)(2,1)} %rays_ref.1, s32[2,1,16]{2,1,0:T(1,128)} %bitcast.12, s32[2,1,16]{2,1,0:T(1,128)} %bitcast.13, f32[3,1,3]{2,1,0:T(1,128)} %bitcast.11), custom_call_target="tpu_custom_call" | custom-call | tf_op jit(solution)/shard_map/prepare/pallas_call | solution.py:343
  1.8 5.1 %collective-permute-start.8 = (bf16[1,184,256]{2,1,0:T(8,128)(2,1)S(1)}, bf16[1,184,256]{2,1,0:T(8,128)(2,1)S(1)}, u32[]{:S(2)}, u32[]{:S(2)}) collective-permute-start(bf16[1,184,256]{2,1,0:T(8,128)(2,1)S(1)} %get-tuple-element.15.refs_2_), channel_id=1, source_target_pairs={{0,24},{1,25},{2,26},{3,27},{4,28},{5,29},{6,30},{7,31},{8,16},{9,... | collective-permute-start | bytes 282632 | tf_op jit(solution)/shard_map/ppermute | solution.py:337
  6.9 0.0 collective-permute-start.7
  6.9 0.0 collective-permute-start.2
  6.9 0.7 %collective-permute-start.4 = (bf16[1,184,256]{2,1,0:T(8,128)(2,1)S(1)}, bf16[1,184,256]{2,1,0:T(8,128)(2,1)S(1)}, u32[]{:S(2)}, u32[]{:S(2)}) collective-permute-start(bf16[1,184,256]{2,1,0:T(8,128)(2,1)S(1)} %get-tuple-element.15.refs_2_), channel_id=1, source_target_pairs={{0,16},{1,17},{2,18},{3,19},{4,20},{5,21},{6,22},{7,23},{8,24},{9,... | collective-permute-start | bytes 282632 | tf_op jit(solution)/shard_map/ppermute | solution.py:337
  7.6 2.5 %collective-permute-start.6 = (bf16[1,368,256]{2,1,0:T(8,128)(2,1)S(1)}, bf16[1,368,256]{2,1,0:T(8,128)(2,1)S(1)}, u32[]{:S(2)}, u32[]{:S(2)}) collective-permute-start(bf16[1,368,256]{2,1,0:T(8,128)(2,1)S(1)} %get-tuple-element.14.refs_0_.refs_13_), channel_id=1, source_target_pairs={{0,5},{1,4},{2,7},{3,6},{4,1},{5,0},{6,3},{7,2},{8,13},{9,12},{10,... | collective-permute-start | bytes 565256 | tf_op jit(solution)/shard_map/ppermute | solution.py:337
  10.1 0.3 collective-permute-done.8.refs_4_
  10.4 0.0 collective-permute-start.9
  10.4 0.0 collective-permute-done.7.refs_3_
  10.4 1.6 %collective-permute-start = (bf16[1,368,256]{2,1,0:T(8,128)(2,1)S(1)}, bf16[1,368,256]{2,1,0:T(8,128)(2,1)S(1)}, u32[]{:S(2)}, u32[]{:S(2)}) collective-permute-start(bf16[1,368,256]{2,1,0:T(8,128)(2,1)S(1)} %get-tuple-element.14.refs_0_.refs_13_), channel_id=1, source_target_pairs={{0,1},{1,0},{2,3},{3,2},{4,5},{5,4},{6,7},{7,6},{8,9},{9,8},{10,11... | collective-permute-start | bytes 565256 | tf_op jit(solution)/shard_map/ppermute | solution.py:337
  12.0 1.5 %collective-permute-done.2.refs_2_ = bf16[1,184,256]{2,1,0:T(8,128)(2,1)S(1)} collective-permute-done((bf16[1,184,256]{2,1,0:T(8,128)(2,1)S(1)}, bf16[1,184,256]{2,1,0:T(8,128)(2,1)S(1)}, u32[]{:S(2)}, u32[]{:S(2)}) %collective-permute-start.2) | collective-permute-done | bytes 94240 | tf_op jit(solution)/shard_map/ppermute | solution.py:337
  13.5 1.5 %collective-permute-start.1 = (bf16[1,368,256]{2,1,0:T(8,128)(2,1)S(1)}, bf16[1,368,256]{2,1,0:T(8,128)(2,1)S(1)}, u32[]{:S(2)}, u32[]{:S(2)}) collective-permute-start(bf16[1,368,256]{2,1,0:T(8,128)(2,1)S(1)} %get-tuple-element.14.refs_0_.refs_13_), channel_id=1, source_target_pairs={{0,4},{1,5},{2,6},{3,7},{4,0},{5,1},{6,2},{7,3},{8,12},{9,13},{10,... | collective-permute-start | bytes 565256 | tf_op jit(solution)/shard_map/ppermute | solution.py:337
  15.0 0.0 collective-permute-done.4.refs_4_
  15.0 0.0 collective-permute-start.3
  15.0 0.0 collective-permute-done.9.refs_5_
  15.0 0.5 %collective-permute-start.5 = (bf16[1,184,256]{2,1,0:T(8,128)(2,1)S(1)}, bf16[1,184,256]{2,1,0:T(8,128)(2,1)S(1)}, u32[]{:S(2)}, u32[]{:S(2)}) collective-permute-start(bf16[1,184,256]{2,1,0:T(8,128)(2,1)S(1)} %collective-permute-done.4.refs_4_), channel_id=1, source_target_pairs={{0,2},{1,3},{2,0},{3,1},{4,6},{5,7},{6,4},{7,5},{8,10},{9,11},{10,... | collective-permute-start | bytes 282632 | tf_op jit(solution)/shard_map/ppermute | solution.py:337
  15.5 0.8 %early.1 = (bf16[2,368,256]{2,1,0:T(8,128)(2,1)S(1)}, f32[2,360,256]{2,1,0:T(8,128)S(1)}, f32[2,256]{1,0:T(2,128)S(1)}, bf16[4,192,256]{2,1,0:T(8,128)(2,1)S(1)}...) custom-call(bf16[1,368,256]{2,1,0:T(8,128)(2,1)S(1)} %get-tuple-element.14.refs_0_.refs_13_, ...), custom_call_target="tpu_custom_call" | custom-call | tf_op jit(solution)/shard_map/early/pallas_call | solution.py:382
  16.3 0.0 collective-permute-done.3.refs_3_
  16.3 0.2 collective-permute-done.5.refs_5_
  16.4 2.6 %collective-permute-done.refs_0_ = bf16[1,368,256]{2,1,0:T(8,128)(2,1)S(1)} collective-permute-done((bf16[1,368,256]{2,1,0:T(8,128)(2,1)S(1)}, bf16[1,368,256]{2,1,0:T(8,128)(2,1)S(1)}, u32[]{:S(2)}, u32[]{:S(2)}) %collective-permute-start) | collective-permute-done | bytes 188448 | tf_op jit(solution)/shard_map/ppermute | solution.py:337
  19.1 0.9 %collective-permute-done.1.refs_1_ = bf16[1,368,256]{2,1,0:T(8,128)(2,1)S(1)} collective-permute-done((bf16[1,368,256]{2,1,0:T(8,128)(2,1)S(1)}, bf16[1,368,256]{2,1,0:T(8,128)(2,1)S(1)}, u32[]{:S(2)}, u32[]{:S(2)}) %collective-permute-start.1) | collective-permute-done | bytes 188448 | tf_op jit(solution)/shard_map/ppermute | solution.py:337
  20.0 1.6 %last.1 = f32[32,1,128]{2,1,0:T(1,128)S(1)} custom-call(bf16[1,368,256]{2,1,0:T(8,128)(2,1)S(1)} %collective-permute-done.refs_0_, bf16[1,368,256]{2,1,0:T(8,128)(2,1)S(1)} %collective-permute-done.1.refs_1_, bf16[1,184,256]{2,1,0:T(8,128)(2,1)S(1)} %collective-permute-done.2.refs_2_, bf16[1,184,256]{2,1,0:T(8,128)(2,1)S(1)} %collective-permute-done.3.refs_3_, ...), custom_call_target="tpu_custom_call" | custom-call | tf_op jit(solution)/shard_map/last/pallas_call | solution.py:393
  21.6 12.1 %all_to_all.5.gathered_ref = f32[32,1,128]{2,1,0:T(1,128)S(1)} all-to-all(f32[32,1,128]{2,1,0:T(1,128)S(1)} %last.1), channel_id=1, replica_groups=mesh['row'=16,'col'=2] {'row','col'}, dimensions={0} | all-to-all | bytes 32768 | tf_op jit(solution)/shard_map/all_to_all | solution.py:410
  33.7 1.9 %power.1 = (f32[2,1,16]{2,1,0:T(1,128)}, f32[3,1,3]{2,1,0:T(1,128)}) custom-call(f32[32,1,128]{2,1,0:T(1,128)S(1)} %all_to_all.5.gathered_ref), custom_call_target="tpu_custom_call" | custom-call | tf_op jit(solution)/shard_map/power/pallas_call | solution.py:412
  (1 shorter events, 0.0 us)
Async XLA Ops:
  1.8 8.7 %collective-permute-start.8 = (bf16[1,184,256]{2,1,0:T(8,128)(2,1)S(1)}, bf16[1,184,256]{2,1,0:T(8,128)(2,1)S(1)}, u32[]{:S(2)}, u32[]{:S(2)}) collective-permute-start(bf16[1,184,256]{2,1,0:T(8,128)(2,1)S(1)} %get-tuple-element.15.refs_2_), channel_id=1, source_target_pairs={{0,24},{1,25},{2,26},{3,27},{4,28},{5,29},{6,30},{7,31},{8,16},{9,... | collective-permute-start | bytes 282632 | tf_op jit(solution)/shard_map/ppermute | solution.py:337
  6.9 3.5 %collective-permute-start.7 = (bf16[1,184,256]{2,1,0:T(8,128)(2,1)S(1)}, bf16[1,184,256]{2,1,0:T(8,128)(2,1)S(1)}, u32[]{:S(2)}, u32[]{:S(2)}) collective-permute-start(bf16[1,184,256]{2,1,0:T(8,128)(2,1)S(1)} %get-tuple-element.15.refs_2_), channel_id=1, source_target_pairs={{0,2},{1,3},{2,0},{3,1},{4,6},{5,7},{6,4},{7,5},{8,10},{9,11},{10,... | collective-permute-start | bytes 282632 | tf_op jit(solution)/shard_map/ppermute | solution.py:337
  6.9 6.6 %collective-permute-start.2 = (bf16[1,184,256]{2,1,0:T(8,128)(2,1)S(1)}, bf16[1,184,256]{2,1,0:T(8,128)(2,1)S(1)}, u32[]{:S(2)}, u32[]{:S(2)}) collective-permute-start(bf16[1,184,256]{2,1,0:T(8,128)(2,1)S(1)} %get-tuple-element.15.refs_2_), channel_id=1, source_target_pairs={{0,8},{1,9},{2,10},{3,11},{4,12},{5,13},{6,14},{7,15},{8,0},{9,1},... | collective-permute-start | bytes 282632 | tf_op jit(solution)/shard_map/ppermute | solution.py:337
  6.9 8.1 %collective-permute-start.4 = (bf16[1,184,256]{2,1,0:T(8,128)(2,1)S(1)}, bf16[1,184,256]{2,1,0:T(8,128)(2,1)S(1)}, u32[]{:S(2)}, u32[]{:S(2)}) collective-permute-start(bf16[1,184,256]{2,1,0:T(8,128)(2,1)S(1)} %get-tuple-element.15.refs_2_), channel_id=1, source_target_pairs={{0,16},{1,17},{2,18},{3,19},{4,20},{5,21},{6,22},{7,23},{8,24},{9,... | collective-permute-start | bytes 282632 | tf_op jit(solution)/shard_map/ppermute | solution.py:337
  7.6 7.9 %collective-permute-start.6 = (bf16[1,368,256]{2,1,0:T(8,128)(2,1)S(1)}, bf16[1,368,256]{2,1,0:T(8,128)(2,1)S(1)}, u32[]{:S(2)}, u32[]{:S(2)}) collective-permute-start(bf16[1,368,256]{2,1,0:T(8,128)(2,1)S(1)} %get-tuple-element.14.refs_0_.refs_13_), channel_id=1, source_target_pairs={{0,5},{1,4},{2,7},{3,6},{4,1},{5,0},{6,3},{7,2},{8,13},{9,12},{10,... | collective-permute-start | bytes 565256 | tf_op jit(solution)/shard_map/ppermute | solution.py:337
  10.4 4.6 %collective-permute-start.9 = (bf16[1,184,256]{2,1,0:T(8,128)(2,1)S(1)}, bf16[1,184,256]{2,1,0:T(8,128)(2,1)S(1)}, u32[]{:S(2)}, u32[]{:S(2)}) collective-permute-start(bf16[1,184,256]{2,1,0:T(8,128)(2,1)S(1)} %collective-permute-done.8.refs_4_), channel_id=1, source_target_pairs={{0,2},{1,3},{2,0},{3,1},{4,6},{5,7},{6,4},{7,5},{8,10},{9,11},{10,... | collective-permute-start | bytes 282632 | tf_op jit(solution)/shard_map/ppermute | solution.py:337
  10.4 8.6 %collective-permute-start = (bf16[1,368,256]{2,1,0:T(8,128)(2,1)S(1)}, bf16[1,368,256]{2,1,0:T(8,128)(2,1)S(1)}, u32[]{:S(2)}, u32[]{:S(2)}) collective-permute-start(bf16[1,368,256]{2,1,0:T(8,128)(2,1)S(1)} %get-tuple-element.14.refs_0_.refs_13_), channel_id=1, source_target_pairs={{0,1},{1,0},{2,3},{3,2},{4,5},{5,4},{6,7},{7,6},{8,9},{9,8},{10,11... | collective-permute-start | bytes 565256 | tf_op jit(solution)/shard_map/ppermute | solution.py:337
  13.5 6.5 %collective-permute-start.1 = (bf16[1,368,256]{2,1,0:T(8,128)(2,1)S(1)}, bf16[1,368,256]{2,1,0:T(8,128)(2,1)S(1)}, u32[]{:S(2)}, u32[]{:S(2)}) collective-permute-start(bf16[1,368,256]{2,1,0:T(8,128)(2,1)S(1)} %get-tuple-element.14.refs_0_.refs_13_), channel_id=1, source_target_pairs={{0,4},{1,5},{2,6},{3,7},{4,0},{5,1},{6,2},{7,3},{8,12},{9,13},{10,... | collective-permute-start | bytes 565256 | tf_op jit(solution)/shard_map/ppermute | solution.py:337
  15.0 1.3 %collective-permute-start.3 = (bf16[1,184,256]{2,1,0:T(8,128)(2,1)S(1)}, bf16[1,184,256]{2,1,0:T(8,128)(2,1)S(1)}, u32[]{:S(2)}, u32[]{:S(2)}) collective-permute-start(bf16[1,184,256]{2,1,0:T(8,128)(2,1)S(1)} %collective-permute-done.2.refs_2_), channel_id=1, source_target_pairs={{0,2},{1,3},{2,0},{3,1},{4,6},{5,7},{6,4},{7,5},{8,10},{9,11},{10,... | collective-permute-start | bytes 282632 | tf_op jit(solution)/shard_map/ppermute | solution.py:337
  15.0 1.4 %collective-permute-start.5 = (bf16[1,184,256]{2,1,0:T(8,128)(2,1)S(1)}, bf16[1,184,256]{2,1,0:T(8,128)(2,1)S(1)}, u32[]{:S(2)}, u32[]{:S(2)}) collective-permute-start(bf16[1,184,256]{2,1,0:T(8,128)(2,1)S(1)} %collective-permute-done.4.refs_4_), channel_id=1, source_target_pairs={{0,2},{1,3},{2,0},{3,1},{4,6},{5,7},{6,4},{7,5},{8,10},{9,11},{10,... | collective-permute-start | bytes 282632 | tf_op jit(solution)/shard_map/ppermute | solution.py:337

commit v3 on v2

--- a/solution.py
+++ b/solution.py
@@ -43,19 +43,19 @@
 ):
     rays, depth = rays_ref.shape[1:]
     half = half_ref.shape[1]
-    moves = (
-        (rays_ref.at[:, pl.ds(0, half)], half_ref),
-        (rays_ref.at[:, pl.ds(0, half)], full_ref.at[:, pl.ds(0, half)]),
-        (rays_ref.at[:, pl.ds(half, rays - half)], full_ref.at[:, pl.ds(half, rays - half)]),
-        (first_ref, first_row),
-        (second_ref, second_row),
-        (start_ref, frame_ref),
-    )
+    cuts = [0, half // 16 * 8, half, half + (rays - half) // 16 * 8, rays]
+    moves = [
+        (rays_ref.at[:, pl.ds(low, high - low)], to.at[:, pl.ds(low, high - low)])
+        for low, high, to in zip(cuts, cuts[1:], (half_ref, half_ref, full_ref, full_ref))
+    ]
+    moves += [(first_ref, first_row), (second_ref, second_row), (start_ref, frame_ref)]
     copies = [pltpu.make_async_copy(*move, sems.at[k]) for k, move in enumerate(moves)]
     for copy in copies:
         copy.start()
     for copy in copies:
         copy.wait()
+
+    full_ref[0, :half] = half_ref[0]
 
     def row(table_ref):
         parts = [table_ref[c] for c in range(plan.cols)]
@@ -165,58 +165,65 @@
     return jnp.sum(placed, axis=0, keepdims=True)
 
 
-def early_kernel(rays, half, ns, ms, *refs):
+def early_kernel(plan, rays, half, ns, ms, loaded, *refs):
     firsts, refs = refs[: len(ns)], refs[len(ns) :]
-    seconds, refs = refs[: len(ms)], refs[len(ms) :]
-    first_stack, first_rows, first_sum, second_stack, second_rows, second_sum, stats, means, parts = refs
+    if loaded:
+        second_stack, second_sum, own_ref, start_ref = refs[:4]
+        first_stack, first_rows, first_sum, stats, index_ref, base_ref, means, parts = refs[4:]
+        tables = (ref[0, rays : rays + TABLE] for ref in (own_ref, firsts[ns.index(plan.cols)]))
+        paired, sent = lines(plan, *tables)
+        index_ref[0:1, : plan.pairs] = paired[0].astype(jnp.int32)
+        index_ref[1:2, : plan.pairs] = paired[1].astype(jnp.int32)
+        spare = plan.width - 3 * plan.pairs - 9
+        base_ref[...] = jnp.concatenate(
+            [jnp.zeros((1, plan.pairs), jnp.float32), *sent, *(start_ref[k] for k in range(3))]
+            + [jnp.zeros((1, spare), jnp.float32)] * (spare > 0),
+            axis=1,
+        )
+        second_sums = [second_sum[m : m + 1] for m in range(len(ms))]
+    else:
+        seconds, refs = refs[: len(ms)], refs[len(ms) :]
+        first_stack, first_rows, first_sum, stats, second_stack, second_rows, second_sum, means, parts = refs
+        second_sums = load_seconds(seconds, half, second_stack, second_rows)
+        second_sum[...] = jnp.concatenate(second_sums, axis=0)
     first_sums = load_firsts(firsts, first_stack, first_rows)
-    second_sums = load_seconds(seconds, half, second_stack, second_rows)
     first_sum[...] = jnp.concatenate(first_sums, axis=0)
-    second_sum[...] = jnp.concatenate(second_sums, axis=0)
     centers, spreads = cross(rays, half, first_stack, second_stack, first_sums, second_sums, means, parts)
     for n in range(len(ns)):
         stats[0, n] = jnp.broadcast_to(centers[n], (len(ms), LANES))
         stats[1, n] = jnp.broadcast_to(spreads[n], (len(ms), LANES))
 
 
-def last_kernel(plan, rays, half, early, late, *refs):
-    ns, ms = late
+def last_kernel(plan, rays, half, groups, early, ns, ms, *refs):
     firsts, refs = refs[: len(ns)], refs[len(ns) :]
     seconds, refs = refs[: len(ms)], refs[len(ms) :]
-    early_firsts, early_rows, early_sum, early_seconds, early_second_rows, early_second_sum = refs[:6]
-    early_stats, own_ref, start_ref, message_ref, index_row, index, sem = refs[6:13]
-    first_stack, first_rows, second_stack, second_rows, means, parts, picked_first, picked_second = refs[13:]
-    own_table = own_ref[0, rays : rays + TABLE]
-    next_table = firsts[ns.index(plan.cols)][0, rays : rays + TABLE]
-    paired, sent = lines(plan, own_table, next_table)
-    index_row[0:1, : plan.pairs] = paired[0].astype(jnp.int32)
-    index_row[1:2, : plan.pairs] = paired[1].astype(jnp.int32)
-    copy = pltpu.make_async_copy(index_row, index, sem)
+    before, refs = [refs[4 * g : 4 * g + 4] for g in range(len(groups))], refs[4 * len(groups) :]
+    early_seconds, early_second_rows, early_second_sum = refs[:3]
+    index_ref, base_ref, message_ref, index, sem = refs[3:8]
+    first_stack, first_rows, second_stack, second_rows, means, parts, picked_first, picked_second = refs[8:]
+    copy = pltpu.make_async_copy(index_ref, index, sem)
     copy.start()
+    second_sums = load_seconds(seconds, half, second_stack, second_rows)
     first_sums = load_firsts(firsts, first_stack, first_rows)
-    second_sums = load_seconds(seconds, half, second_stack, second_rows)
-    old_first_sums = [early_sum[n : n + 1] for n in range(len(early[0]))]
-    old_second_sums = [early_second_sum[m : m + 1] for m in range(len(early[1]))]
-    blocks = (
-        (ns, early[1], first_rows, early_second_rows),
-        (early[0], ms, early_rows, second_rows),
-        (ns, ms, first_rows, second_rows),
-        (early[0], early[1], early_rows, early_second_rows),
-    )
-    arrays = (
-        (first_stack, early_seconds, first_sums, old_second_sums),
-        (early_firsts, second_stack, old_first_sums, second_sums),
-        (first_stack, second_stack, first_sums, second_sums),
-    )
-    stats = [cross(rays, half, *arrays[k], means.at[k], parts.at[k]) for k in range(3)]
-    stats.append([[early_stats[kind, n][:, 0:1] for n in range(len(early[0]))] for kind in range(2)])
+    old_second_sums = [early_second_sum[m : m + 1] for m in range(len(early))]
+
+    blocks, stats = [], []
+
+    def block(one, two, one_stack, two_stack, one_sums, two_sums, one_rows, two_rows):
+        k = len(blocks)
+        stats.append(cross(rays, half, one_stack, two_stack, one_sums, two_sums, means.at[k], parts.at[k]))
+        blocks.append((one, two, one_rows, two_rows))
+
+    for group, (stack, rows, sums, _) in zip(groups, before):
+        old_sums = [sums[n : n + 1] for n in range(len(group))]
+        block(group, ms, stack, second_stack, old_sums, second_sums, rows, second_rows)
+    block(ns, early, first_stack, early_seconds, first_sums, old_second_sums, first_rows, early_second_rows)
+    block(ns, ms, first_stack, second_stack, first_sums, second_sums, first_rows, second_rows)
+    for group, (_, rows, _, old) in zip(groups, before):
+        stats.append([[old[kind, n][:, 0:1] for n in range(len(group))] for kind in range(2)])
+        blocks.append((group, early, rows, early_second_rows))
     copy.wait()
-    spare = plan.width - 3 * plan.pairs - 9
-    message = jnp.concatenate(
-        [jnp.zeros((1, plan.pairs), jnp.float32), *sent, *(start_ref[k] for k in range(3))]
-        + [jnp.zeros((1, spare), jnp.float32)] * (spare > 0),
-        axis=1,
-    )
+    message = base_ref[...]
     for k, (one, two, one_rows, two_rows) in enumerate(blocks):
         message = message + place(
             plan, one, two, *stats[k], one_rows, two_rows, index, picked_first.at[k], picked_second.at[k]
@@ -352,7 +359,7 @@
         scratch_shapes=[
             pltpu.VMEM(first.shape, first.dtype),
             pltpu.VMEM(second.shape, second.dtype),
-            pltpu.SemaphoreType.DMA((6,)),
+            pltpu.SemaphoreType.DMA((7,)),
         ],
         compiler_params=pltpu.CompilerParams(vmem_limit_bytes=1 << 20),
         name="prepare",
@@ -365,47 +372,64 @@
 
     first_height, second_height = -(-rays // 16) * 16, -(-half // 16) * 16
     params = pltpu.CompilerParams(vmem_limit_bytes=SCORE_VMEM)
-    (early_ns, early_ms), (late_ns, late_ms) = early_part(plan), late_part(plan)
-
-    def stacks(ns, ms):
+    groups, late_ns = first_groups(plan)
+    early_ms, late_ms = second_groups(plan)
+
+    def first_shapes(ns):
         return [
             ((len(ns), first_height, depth), polar_rays.dtype),
             ((len(ns), rays, depth), jnp.float32),
             ((len(ns), depth), jnp.float32),
+        ]
+
+    def second_shapes(ms):
+        return [
             ((len(ms), second_height, depth), polar_rays.dtype),
             ((len(ms), half, depth), jnp.float32),
             ((len(ms), depth), jnp.float32),
         ]
 
     most = max(len(early_ms), len(late_ms))
-    span = max(len(early_ns), len(late_ns)) * first_height
-    before = pl.pallas_call(
-        functools.partial(early_kernel, rays, half, early_ns, early_ms),
-        out_shape=[jax.ShapeDtypeStruct(*one) for one in stacks(early_ns, early_ms)]
-        + [jax.ShapeDtypeStruct((2, len(early_ns), len(early_ms), LANES), jnp.float32)],
-        in_specs=[vmem] * (len(early_ns) + len(early_ms)),
-        out_specs=[vmem] * 7,
-        compiler_params=params,
-        scratch_shapes=[pltpu.VMEM((most, span), jnp.float32)] * 2,
-        name="early",
-    )(*(fulls[n] for n in early_ns), *(halves[m] for m in early_ms))
-    new = stacks(late_ns, late_ms)
+    span = max(len(ns) for ns in (*groups, late_ns)) * first_height
+    before, seconds = [], None
+    for ns in groups:
+        shapes = first_shapes(ns) + [((2, len(ns), len(early_ms), LANES), jnp.float32)]
+        inputs = [fulls[n] for n in ns]
+        if seconds is None:
+            shapes += second_shapes(early_ms)
+            inputs += [halves[m] for m in early_ms]
+        else:
+            shapes += [((2, plan.index), jnp.int32), ((1, plan.width), jnp.float32)]
+            inputs += [seconds[0], seconds[2], own_rays, own_frame]
+        outs = pl.pallas_call(
+            functools.partial(early_kernel, plan, rays, half, ns, early_ms, seconds is not None),
+            out_shape=[jax.ShapeDtypeStruct(*one) for one in shapes],
+            in_specs=[vmem] * len(inputs),
+            out_specs=[vmem] * len(shapes),
+            compiler_params=params,
+            scratch_shapes=[pltpu.VMEM((most, span), jnp.float32)] * 2,
+        )(*inputs)
+        before += list(outs[:4])
+        seconds = seconds or list(outs[4:])
+    index, base = outs[4:]
+    inputs = [fulls[n] for n in late_ns] + [halves[m] for m in late_ms] + before + seconds
+    inputs += [index, base]
+    kinds = 2 * len(groups) + 2
     message = pl.pallas_call(
-        functools.partial(last_kernel, plan, rays, half, (early_ns, early_ms), (late_ns, late_ms)),
+        functools.partial(last_kernel, plan, rays, half, groups, early_ms, late_ns, late_ms),
         out_shape=jax.ShapeDtypeStruct((plan.count, 1, plan.width), jnp.float32),
-        in_specs=[vmem] * (len(late_ns) + len(late_ms) + 9),
+        in_specs=[vmem] * len(inputs),
         out_specs=vmem,
         compiler_params=params,
         scratch_shapes=[
-            pltpu.VMEM((2, plan.index), jnp.int32),
             pltpu.SMEM((2, plan.index), jnp.int32),
             pltpu.SemaphoreType.DMA,
         ]
-        + [pltpu.VMEM(*one) for one in (new[0], new[1], new[3], new[4])]
-        + [pltpu.VMEM((3, most, span), jnp.float32)] * 2
-        + [pltpu.VMEM((4, most, depth), jnp.float32)] * 2,
+        + [pltpu.VMEM(*one) for one in first_shapes(late_ns)[:2] + second_shapes(late_ms)[:2]]
+        + [pltpu.VMEM((kinds, most, span), jnp.float32)] * 2
+        + [pltpu.VMEM((kinds, most, depth), jnp.float32)] * 2,
         name="last",
-    )(*(fulls[n] for n in late_ns), *(halves[m] for m in late_ms), *before, own_rays, own_frame)
+    )(*inputs)
 
     gathered = lax.all_to_all(message, axes, 0, 0, tiled=True)
 
@@ -432,17 +456,15 @@
     return scored(plan, *arrays)
 
 
-def early_part(plan):
-    deep = [0] + list(range(plan.depth - 1, plan.depth // 2, -1))
-    return (0, plan.firsts - 1), tuple(PAIR * dz + dk for dz in deep for dk in range(PAIR))
-
-
-def late_part(plan):
-    ns, ms = early_part(plan)
-    return (
-        tuple(n for n in range(plan.firsts) if n not in ns),
-        tuple(m for m in range(plan.seconds) if m not in ms),
-    )
+def first_groups(plan):
+    middle = range(plan.firsts - 2, 0, -1)
+    cut = len(middle) // 2
+    return ((0, plan.firsts - 1), tuple(middle[:cut])), tuple(middle[cut:])
+
+
+def second_groups(plan):
+    far = plan.depth - 1
+    return tuple(range(PAIR * far)), tuple(range(PAIR * far, plan.seconds))
 
 
 def solution(mesh):

time: 35.8 us -> 37.1 us (1.036)
  blocking collectives: 12.1 us -> 13.6 us
  starting transfers between devices: 12 us -> 10.9 us
  waiting for transfers between devices: 5.48 us -> 5.95 us
    all_to_all x1, blocking collectives: 12.1 us -> 13.6 us  [scored(): gathered = lax.all_to_all(message, axes, 0, 0, tiled=True)]
    ppermute x10, starting transfers between devices: 12 us -> 10.9 us  [swap(): lax.ppermute(value, axes, [(n, n ^ distance) for n in range(plan.count)])]
    ppermute x10, waiting for transfers between devices: 5.48 us -> 5.95 us  [swap(): lax.ppermute(value, axes, [(n, n ^ distance) for n in range(plan.count)])]
    pallas_call x2 -> x3, Pallas kernels: 2.4 us -> 2.84 us  [the longest x2 1.61 us: scored(): pl.pallas_call(functools.partial(early_kernel, plan, rays, half, ns, earl...]
  transfers between devices with their start and end apart: 10 -> 10, of which waited for: 5 -> 5; matrix products, arithmetic and copies ran while one was open for 0% -> 0% of each run, Pallas kernels for 2% -> 4%
where the time goes in v3:
time: 37.1 us; the launch traced here: 36.9 us
  blocking collectives  13.6 us (37%)
  starting transfers between devices  10.9 us (29%)
  waiting for transfers between devices  5.95 us (16%)
  Pallas kernels  5.7 us (15%)
  between operations  0.67 us (2%)
    all_to_all x1, blocking collectives, scored(): gathered = lax.all_to_all(message, axes, 0, 0, tiled=True)  13.6 us
    ppermute x10, starting transfers between devices, swap(): lax.ppermute(value, axes, [(n, n ^ distance) for n in range(plan.count)])  10.9 us
    ppermute x10, waiting for transfers between devices, swap(): lax.ppermute(value, axes, [(n, n ^ distance) for n in range(plan.count)])  5.95 us
    pallas_call x1, Pallas kernels, scored(): pl.pallas_call(functools.partial(power_kernel, plan, rays), out_shape=(ja...  1.85 us
    pallas_call x2, Pallas kernels, scored(): pl.pallas_call(functools.partial(early_kernel, plan, rays, half, ns, earl...  1.61 us
    pallas_call x1, Pallas kernels, scored(): pl.pallas_call(functools.partial(last_kernel, plan, rays, half, groups, e...  1.23 us
    pallas_call x1, Pallas kernels, scored(): pl.pallas_call(functools.partial(prepare_kernel, plan), out_shape=(jax.Sh...  1.01 us
  transfers between devices with their start and end apart: 10, of which 5 were waited for; matrix products, arithmetic and copies ran while one was open for 0% of the time, Pallas kernels for 4%

profile of v3, /device:TPU:0, one launch (start us, length us, event | category | flops | bytes accessed | tf_op | source)
XLA Modules:
  0.0 36.9 jit_solution(17794942979998860119)
XLA Ops:
  0.6 1.0 %prepare.1 = (bf16[1,368,256]{2,1,0:T(8,128)(2,1)S(1)}, bf16[1,184,256]{2,1,0:T(8,128)(2,1)S(1)}, f32[3,1,3]{2,1,0:T(1,128)S(1)}) custom-call(bf16[1,360,256]{2,1,0:T(8,128)(2,1)} %rays_ref.1, s32[2,1,16]{2,1,0:T(1,128)} %bitcast.12, s32[2,1,16]{2,1,0:T(1,128)} %bitcast.13, f32[3,1,3]{2,1,0:T(1,128)} %bitcast.11), custom_call_target="tpu_custom_call" | custom-call | tf_op jit(solution)/shard_map/prepare/pallas_call | solution.py:350
  1.6 3.1 %collective-permute-start.5 = (bf16[1,184,256]{2,1,0:T(8,128)(2,1)S(1)}, bf16[1,184,256]{2,1,0:T(8,128)(2,1)S(1)}, u32[]{:S(2)}, u32[]{:S(2)}) collective-permute-start(bf16[1,184,256]{2,1,0:T(8,128)(2,1)S(1)} %get-tuple-element.21.refs_2_), channel_id=1, source_target_pairs={{0,8},{1,9},{2,10},{3,11},{4,12},{5,13},{6,14},{7,15},{8,0},{9,1},... | collective-permute-start | bytes 282632 | tf_op jit(solution)/shard_map/ppermute | solution.py:344
  4.8 2.6 %collective-permute-start.7 = (bf16[1,184,256]{2,1,0:T(8,128)(2,1)S(1)}, bf16[1,184,256]{2,1,0:T(8,128)(2,1)S(1)}, u32[]{:S(2)}, u32[]{:S(2)}) collective-permute-start(bf16[1,184,256]{2,1,0:T(8,128)(2,1)S(1)} %get-tuple-element.21.refs_2_), channel_id=1, source_target_pairs={{0,16},{1,17},{2,18},{3,19},{4,20},{5,21},{6,22},{7,23},{8,24},{9,... | collective-permute-start | bytes 282632 | tf_op jit(solution)/shard_map/ppermute | solution.py:344
  7.4 0.0 collective-permute-start.4
  7.4 0.0 collective-permute-start.1
  7.4 2.7 %collective-permute-start.3 = (bf16[1,368,256]{2,1,0:T(8,128)(2,1)S(1)}, bf16[1,368,256]{2,1,0:T(8,128)(2,1)S(1)}, u32[]{:S(2)}, u32[]{:S(2)}) collective-permute-start(bf16[1,368,256]{2,1,0:T(8,128)(2,1)S(1)} %get-tuple-element.20.refs_0_.refs_3_), channel_id=1, source_target_pairs={{0,5},{1,4},{2,7},{3,6},{4,1},{5,0},{6,3},{7,2},{8,13},{9,12},{10,... | collective-permute-start | bytes 565256 | tf_op jit(solution)/shard_map/ppermute | solution.py:344
  10.0 0.0 collective-permute-done.5.refs_4_
  10.0 0.5 %collective-permute-start.9 = (bf16[1,368,256]{2,1,0:T(8,128)(2,1)S(1)}, bf16[1,368,256]{2,1,0:T(8,128)(2,1)S(1)}, u32[]{:S(2)}, u32[]{:S(2)}) collective-permute-start(bf16[1,368,256]{2,1,0:T(8,128)(2,1)S(1)} %get-tuple-element.20.refs_0_.refs_3_), channel_id=1, source_target_pairs={{0,4},{1,5},{2,6},{3,7},{4,0},{5,1},{6,2},{7,3},{8,12},{9,13},{10,... | collective-permute-start | bytes 565256 | tf_op jit(solution)/shard_map/ppermute | solution.py:344
  10.6 1.8 %collective-permute-done.7.refs_6_ = bf16[1,184,256]{2,1,0:T(8,128)(2,1)S(1)} collective-permute-done((bf16[1,184,256]{2,1,0:T(8,128)(2,1)S(1)}, bf16[1,184,256]{2,1,0:T(8,128)(2,1)S(1)}, u32[]{:S(2)}, u32[]{:S(2)}) %collective-permute-start.7) | collective-permute-done | bytes 94240 | tf_op jit(solution)/shard_map/ppermute | solution.py:344
  12.4 0.0 collective-permute-start.6
  12.4 0.0 collective-permute-done.4.refs_3_
  12.4 1.5 %collective-permute-start = (bf16[1,368,256]{2,1,0:T(8,128)(2,1)S(1)}, bf16[1,368,256]{2,1,0:T(8,128)(2,1)S(1)}, u32[]{:S(2)}, u32[]{:S(2)}) collective-permute-start(bf16[1,368,256]{2,1,0:T(8,128)(2,1)S(1)} %get-tuple-element.20.refs_0_.refs_3_), channel_id=1, source_target_pairs={{0,1},{1,0},{2,3},{3,2},{4,5},{5,4},{6,7},{7,6},{8,9},{9,8},{10,11... | collective-permute-start | bytes 565256 | tf_op jit(solution)/shard_map/ppermute | solution.py:344
  13.9 0.5 %collective-permute-done.1.refs_1_ = bf16[1,184,256]{2,1,0:T(8,128)(2,1)S(1)} collective-permute-done((bf16[1,184,256]{2,1,0:T(8,128)(2,1)S(1)}, bf16[1,184,256]{2,1,0:T(8,128)(2,1)S(1)}, u32[]{:S(2)}, u32[]{:S(2)}) %collective-permute-start.1) | collective-permute-done | bytes 94240 | tf_op jit(solution)/shard_map/ppermute | solution.py:344
  14.4 0.0 collective-permute-start.8
  14.4 0.5 %collective-permute-start.2 = (bf16[1,184,256]{2,1,0:T(8,128)(2,1)S(1)}, bf16[1,184,256]{2,1,0:T(8,128)(2,1)S(1)}, u32[]{:S(2)}, u32[]{:S(2)}) collective-permute-start(bf16[1,184,256]{2,1,0:T(8,128)(2,1)S(1)} %collective-permute-done.1.refs_1_), channel_id=1, source_target_pairs={{0,2},{1,3},{2,0},{3,1},{4,6},{5,7},{6,4},{7,5},{8,10},{9,11},{10,... | collective-permute-start | bytes 282632 | tf_op jit(solution)/shard_map/ppermute | solution.py:344
  14.9 0.8 %collective-permute-done.8.refs_7_ = bf16[1,184,256]{2,1,0:T(8,128)(2,1)S(1)} collective-permute-done((bf16[1,184,256]{2,1,0:T(8,128)(2,1)S(1)}, bf16[1,184,256]{2,1,0:T(8,128)(2,1)S(1)}, u32[]{:S(2)}, u32[]{:S(2)}) %collective-permute-start.8) | collective-permute-done | bytes 94240 | tf_op jit(solution)/shard_map/ppermute | solution.py:344
  15.7 0.2 collective-permute-done.3.refs_1_
  15.9 1.0 %shard_map.59 = (bf16[2,368,256]{2,1,0:T(8,128)(2,1)S(1)}, f32[2,360,256]{2,1,0:T(8,128)S(1)}, f32[2,256]{1,0:T(2,128)S(1)}, f32[2,2,6,128]{3,2,1,0:T(8,128)S(1)...) custom-call(bf16[1,368,256]{2,1,0:T(8,128)(2,1)S(1)} %get-tuple-element.20.refs_0_.refs_3_, ...), custom_call_target="tpu_custom_call" | custom-call | tf_op jit(solution)/shard_map/pallas_call | solution.py:404
  16.8 2.7 %collective-permute-done.9.refs_0_ = bf16[1,368,256]{2,1,0:T(8,128)(2,1)S(1)} collective-permute-done((bf16[1,368,256]{2,1,0:T(8,128)(2,1)S(1)}, bf16[1,368,256]{2,1,0:T(8,128)(2,1)S(1)}, u32[]{:S(2)}, u32[]{:S(2)}) %collective-permute-start.9) | collective-permute-done | bytes 188448 | tf_op jit(solution)/shard_map/ppermute | solution.py:344
  19.5 0.7 %shard_map.60 = (bf16[1,368,256]{2,1,0:T(8,128)(2,1)S(1)}, f32[1,360,256]{2,1,0:T(8,128)S(1)}, f32[1,256]{1,0:T(1,128)S(1)}, f32[2,1,6,128]{3,2,1,0:T(8,128)S(1)...) custom-call(bf16[1,368,256]{2,1,0:T(8,128)(2,1)S(1)} %collective-permute-done.9.refs_0_, ...), custom_call_target="tpu_custom_call" | custom-call | tf_op jit(solution)/shard_map/pallas_call | solution.py:404
  20.1 0.0 collective-permute-done.refs_0_
  20.2 1.2 %last.1 = f32[32,1,128]{2,1,0:T(1,128)S(1)} custom-call(bf16[1,368,256]{2,1,0:T(8,128)(2,1)S(1)} %collective-permute-done.refs_0_, bf16[1,184,256]{2,1,0:T(8,128)(2,1)S(1)} %collective-permute-done.1.refs_1_, bf16[1,184,256]{2,1,0:T(8,128)(2,1)S(1)} %collective-permute-done.2.refs_2_, bf16[2,368,256]{2,1,0:T(8,128)(2,1)S(1)} %get-tuple-element.22.refs_3_, ...), custom_call_target="tpu_custom_call" | custom-call | tf_op jit(solution)/shard_map/last/pallas_call | solution.py:418
  21.4 13.6 %all_to_all.5.gathered_ref = f32[32,1,128]{2,1,0:T(1,128)S(1)} all-to-all(f32[32,1,128]{2,1,0:T(1,128)S(1)} %last.1), channel_id=1, replica_groups=mesh['row'=16,'col'=2] {'row','col'}, dimensions={0} | all-to-all | bytes 32768 | tf_op jit(solution)/shard_map/all_to_all | solution.py:434
  35.0 1.9 %power.1 = (f32[2,1,16]{2,1,0:T(1,128)}, f32[3,1,3]{2,1,0:T(1,128)}) custom-call(f32[32,1,128]{2,1,0:T(1,128)S(1)} %all_to_all.5.gathered_ref), custom_call_target="tpu_custom_call" | custom-call | tf_op jit(solution)/shard_map/power/pallas_call | solution.py:436
  (2 shorter events, 0.0 us)
Async XLA Ops:
  1.6 8.4 %collective-permute-start.5 = (bf16[1,184,256]{2,1,0:T(8,128)(2,1)S(1)}, bf16[1,184,256]{2,1,0:T(8,128)(2,1)S(1)}, u32[]{:S(2)}, u32[]{:S(2)}) collective-permute-start(bf16[1,184,256]{2,1,0:T(8,128)(2,1)S(1)} %get-tuple-element.21.refs_2_), channel_id=1, source_target_pairs={{0,8},{1,9},{2,10},{3,11},{4,12},{5,13},{6,14},{7,15},{8,0},{9,1},... | collective-permute-start | bytes 282632 | tf_op jit(solution)/shard_map/ppermute | solution.py:344
  4.8 7.6 %collective-permute-start.7 = (bf16[1,184,256]{2,1,0:T(8,128)(2,1)S(1)}, bf16[1,184,256]{2,1,0:T(8,128)(2,1)S(1)}, u32[]{:S(2)}, u32[]{:S(2)}) collective-permute-start(bf16[1,184,256]{2,1,0:T(8,128)(2,1)S(1)} %get-tuple-element.21.refs_2_), channel_id=1, source_target_pairs={{0,16},{1,17},{2,18},{3,19},{4,20},{5,21},{6,22},{7,23},{8,24},{9,... | collective-permute-start | bytes 282632 | tf_op jit(solution)/shard_map/ppermute | solution.py:344
  7.4 5.0 %collective-permute-start.4 = (bf16[1,184,256]{2,1,0:T(8,128)(2,1)S(1)}, bf16[1,184,256]{2,1,0:T(8,128)(2,1)S(1)}, u32[]{:S(2)}, u32[]{:S(2)}) collective-permute-start(bf16[1,184,256]{2,1,0:T(8,128)(2,1)S(1)} %get-tuple-element.21.refs_2_), channel_id=1, source_target_pairs={{0,2},{1,3},{2,0},{3,1},{4,6},{5,7},{6,4},{7,5},{8,10},{9,11},{10,... | collective-permute-start | bytes 282632 | tf_op jit(solution)/shard_map/ppermute | solution.py:344
  7.4 7.0 %collective-permute-start.1 = (bf16[1,184,256]{2,1,0:T(8,128)(2,1)S(1)}, bf16[1,184,256]{2,1,0:T(8,128)(2,1)S(1)}, u32[]{:S(2)}, u32[]{:S(2)}) collective-permute-start(bf16[1,184,256]{2,1,0:T(8,128)(2,1)S(1)} %get-tuple-element.21.refs_2_), channel_id=1, source_target_pairs={{0,24},{1,25},{2,26},{3,27},{4,28},{5,29},{6,30},{7,31},{8,16},{9,... | collective-permute-start | bytes 282632 | tf_op jit(solution)/shard_map/ppermute | solution.py:344
  7.4 8.5 %collective-permute-start.3 = (bf16[1,368,256]{2,1,0:T(8,128)(2,1)S(1)}, bf16[1,368,256]{2,1,0:T(8,128)(2,1)S(1)}, u32[]{:S(2)}, u32[]{:S(2)}) collective-permute-start(bf16[1,368,256]{2,1,0:T(8,128)(2,1)S(1)} %get-tuple-element.20.refs_0_.refs_3_), channel_id=1, source_target_pairs={{0,5},{1,4},{2,7},{3,6},{4,1},{5,0},{6,3},{7,2},{8,13},{9,12},{10,... | collective-permute-start | bytes 565256 | tf_op jit(solution)/shard_map/ppermute | solution.py:344
  10.0 9.5 %collective-permute-start.9 = (bf16[1,368,256]{2,1,0:T(8,128)(2,1)S(1)}, bf16[1,368,256]{2,1,0:T(8,128)(2,1)S(1)}, u32[]{:S(2)}, u32[]{:S(2)}) collective-permute-start(bf16[1,368,256]{2,1,0:T(8,128)(2,1)S(1)} %get-tuple-element.20.refs_0_.refs_3_), channel_id=1, source_target_pairs={{0,4},{1,5},{2,6},{3,7},{4,0},{5,1},{6,2},{7,3},{8,12},{9,13},{10,... | collective-permute-start | bytes 565256 | tf_op jit(solution)/shard_map/ppermute | solution.py:344
  12.4 2.0 %collective-permute-start.6 = (bf16[1,184,256]{2,1,0:T(8,128)(2,1)S(1)}, bf16[1,184,256]{2,1,0:T(8,128)(2,1)S(1)}, u32[]{:S(2)}, u32[]{:S(2)}) collective-permute-start(bf16[1,184,256]{2,1,0:T(8,128)(2,1)S(1)} %collective-permute-done.5.refs_4_), channel_id=1, source_target_pairs={{0,2},{1,3},{2,0},{3,1},{4,6},{5,7},{6,4},{7,5},{8,10},{9,11},{10,... | collective-permute-start | bytes 282632 | tf_op jit(solution)/shard_map/ppermute | solution.py:344
  12.4 7.8 %collective-permute-start = (bf16[1,368,256]{2,1,0:T(8,128)(2,1)S(1)}, bf16[1,368,256]{2,1,0:T(8,128)(2,1)S(1)}, u32[]{:S(2)}, u32[]{:S(2)}) collective-permute-start(bf16[1,368,256]{2,1,0:T(8,128)(2,1)S(1)} %get-tuple-element.20.refs_0_.refs_3_), channel_id=1, source_target_pairs={{0,1},{1,0},{2,3},{3,2},{4,5},{5,4},{6,7},{7,6},{8,9},{9,8},{10,11... | collective-permute-start | bytes 565256 | tf_op jit(solution)/shard_map/ppermute | solution.py:344
  14.4 1.3 %collective-permute-start.8 = (bf16[1,184,256]{2,1,0:T(8,128)(2,1)S(1)}, bf16[1,184,256]{2,1,0:T(8,128)(2,1)S(1)}, u32[]{:S(2)}, u32[]{:S(2)}) collective-permute-start(bf16[1,184,256]{2,1,0:T(8,128)(2,1)S(1)} %collective-permute-done.7.refs_6_), channel_id=1, source_target_pairs={{0,2},{1,3},{2,0},{3,1},{4,6},{5,7},{6,4},{7,5},{8,10},{9,11},{10,... | collective-permute-start | bytes 282632 | tf_op jit(solution)/shard_map/ppermute | solution.py:344
  14.4 5.8 %collective-permute-start.2 = (bf16[1,184,256]{2,1,0:T(8,128)(2,1)S(1)}, bf16[1,184,256]{2,1,0:T(8,128)(2,1)S(1)}, u32[]{:S(2)}, u32[]{:S(2)}) collective-permute-start(bf16[1,184,256]{2,1,0:T(8,128)(2,1)S(1)} %collective-permute-done.1.refs_1_), channel_id=1, source_target_pairs={{0,2},{1,3},{2,0},{3,1},{4,6},{5,7},{6,4},{7,5},{8,10},{9,11},{10,... | collective-permute-start | bytes 282632 | tf_op jit(solution)/shard_map/ppermute | solution.py:344

commit v4 on v3

--- a/solution.py
+++ b/solution.py
@@ -166,10 +166,23 @@
 
 
 def early_kernel(plan, rays, half, ns, ms, loaded, *refs):
+    *refs, means, parts = refs
     firsts, refs = refs[: len(ns)], refs[len(ns) :]
     if loaded:
-        second_stack, second_sum, own_ref, start_ref = refs[:4]
-        first_stack, first_rows, first_sum, stats, index_ref, base_ref, means, parts = refs[4:]
+        second_stack, second_sum, *refs = refs
+    else:
+        seconds, refs = refs[: len(ms)], refs[len(ms) :]
+    if plan.cols in ns:
+        own_ref, start_ref, *refs = refs
+    first_stack, first_rows, first_sum, stats, *refs = refs
+    if loaded:
+        second_sums = [second_sum[m : m + 1] for m in range(len(ms))]
+    else:
+        second_stack, second_rows, second_sum, *refs = refs
+        second_sums = load_seconds(seconds, half, second_stack, second_rows)
+        second_sum[...] = jnp.concatenate(second_sums, axis=0)
+    if plan.cols in ns:
+        index_ref, base_ref = refs
         tables = (ref[0, rays : rays + TABLE] for ref in (own_ref, firsts[ns.index(plan.cols)]))
         paired, sent = lines(plan, *tables)
         index_ref[0:1, : plan.pairs] = paired[0].astype(jnp.int32)
@@ -180,12 +193,6 @@
             + [jnp.zeros((1, spare), jnp.float32)] * (spare > 0),
             axis=1,
         )
-        second_sums = [second_sum[m : m + 1] for m in range(len(ms))]
-    else:
-        seconds, refs = refs[: len(ms)], refs[len(ms) :]
-        first_stack, first_rows, first_sum, stats, second_stack, second_rows, second_sum, means, parts = refs
-        second_sums = load_seconds(seconds, half, second_stack, second_rows)
-        second_sum[...] = jnp.concatenate(second_sums, axis=0)
     first_sums = load_firsts(firsts, first_stack, first_rows)
     first_sum[...] = jnp.concatenate(first_sums, axis=0)
     centers, spreads = cross(rays, half, first_stack, second_stack, first_sums, second_sums, means, parts)
@@ -372,6 +379,7 @@
 
     first_height, second_height = -(-rays // 16) * 16, -(-half // 16) * 16
     params = pltpu.CompilerParams(vmem_limit_bytes=SCORE_VMEM)
+    early_params = pltpu.CompilerParams(vmem_limit_bytes=SCORE_VMEM)
     groups, late_ns = first_groups(plan)
     early_ms, late_ms = second_groups(plan)
 
@@ -395,23 +403,24 @@
     for ns in groups:
         shapes = first_shapes(ns) + [((2, len(ns), len(early_ms), LANES), jnp.float32)]
         inputs = [fulls[n] for n in ns]
+        inputs += [halves[m] for m in early_ms] if seconds is None else [seconds[0], seconds[2]]
         if seconds is None:
             shapes += second_shapes(early_ms)
-            inputs += [halves[m] for m in early_ms]
-        else:
+        if plan.cols in ns:
             shapes += [((2, plan.index), jnp.int32), ((1, plan.width), jnp.float32)]
-            inputs += [seconds[0], seconds[2], own_rays, own_frame]
+            inputs += [own_rays, own_frame]
         outs = pl.pallas_call(
             functools.partial(early_kernel, plan, rays, half, ns, early_ms, seconds is not None),
             out_shape=[jax.ShapeDtypeStruct(*one) for one in shapes],
             in_specs=[vmem] * len(inputs),
             out_specs=[vmem] * len(shapes),
-            compiler_params=params,
+            compiler_params=early_params,
             scratch_shapes=[pltpu.VMEM((most, span), jnp.float32)] * 2,
         )(*inputs)
         before += list(outs[:4])
-        seconds = seconds or list(outs[4:])
-    index, base = outs[4:]
+        seconds = seconds or list(outs[4:7])
+        if plan.cols in ns:
+            index, base = outs[-2:]
     inputs = [fulls[n] for n in late_ns] + [halves[m] for m in late_ms] + before + seconds
     inputs += [index, base]
     kinds = 2 * len(groups) + 2
@@ -459,7 +468,7 @@
 def first_groups(plan):
     middle = range(plan.firsts - 2, 0, -1)
     cut = len(middle) // 2
-    return ((0, plan.firsts - 1), tuple(middle[:cut])), tuple(middle[cut:])
+    return ((0,), (plan.firsts - 1,), tuple(middle[:cut])), tuple(middle[cut:])
 
 
 def second_groups(plan):

time: 37.1 us -> 35.8 us (0.965)
  waiting for transfers between devices: 5.95 us -> 4.29 us
  blocking collectives: 13.6 us -> 12.3 us
  starting transfers between devices: 10.9 us -> 12.2 us
  Pallas kernels: 5.7 us -> 6.1 us
    ppermute x10, waiting for transfers between devices: 5.95 us -> 4.29 us  [swap(): lax.ppermute(value, axes, [(n, n ^ distance) for n in range(plan.count)])]
    all_to_all x1, blocking collectives: 13.6 us -> 12.3 us  [scored(): gathered = lax.all_to_all(message, axes, 0, 0, tiled=True)]
    ppermute x10, starting transfers between devices: 10.9 us -> 12.2 us  [swap(): lax.ppermute(value, axes, [(n, n ^ distance) for n in range(plan.count)])]
    pallas_call x2 -> x3, Pallas kernels: 1.61 us -> 1.97 us  [scored(): pl.pallas_call(functools.partial(early_kernel, plan, rays, half, ns, earl...]
  transfers between devices with their start and end apart: 10 -> 10, of which waited for: 5 -> 4; matrix products, arithmetic and copies ran while one was open for 0% -> 0% of each run, Pallas kernels for 4% -> 6%
where the time goes in v4:
time: 35.8 us; the launch traced here: 35.6 us
  blocking collectives  12.3 us (34%)
  starting transfers between devices  12.2 us (34%)
  Pallas kernels  6.1 us (17%)
  waiting for transfers between devices  4.29 us (12%)
  between operations  0.67 us (2%)
    all_to_all x1, blocking collectives, scored(): gathered = lax.all_to_all(message, axes, 0, 0, tiled=True)  12.3 us
    ppermute x10, starting transfers between devices, swap(): lax.ppermute(value, axes, [(n, n ^ distance) for n in range(plan.count)])  12.2 us
    ppermute x10, waiting for transfers between devices, swap(): lax.ppermute(value, axes, [(n, n ^ distance) for n in range(plan.count)])  4.29 us
    pallas_call x3, Pallas kernels, scored(): pl.pallas_call(functools.partial(early_kernel, plan, rays, half, ns, earl...  1.97 us
    pallas_call x1, Pallas kernels, scored(): pl.pallas_call(functools.partial(power_kernel, plan, rays), out_shape=(ja...  1.85 us
    pallas_call x1, Pallas kernels, scored(): pl.pallas_call(functools.partial(last_kernel, plan, rays, half, groups, e...  1.27 us
    pallas_call x1, Pallas kernels, scored(): pl.pallas_call(functools.partial(prepare_kernel, plan), out_shape=(jax.Sh...  1.01 us
  transfers between devices with their start and end apart: 10, of which 4 were waited for; matrix products, arithmetic and copies ran while one was open for 0% of the time, Pallas kernels for 6%

profile of v4, /device:TPU:0, one launch (start us, length us, event | category | flops | bytes accessed | tf_op | source)
XLA Modules:
  0.0 35.6 jit_solution(2376471187705509125)
XLA Ops:
  0.6 1.0 %prepare.1 = (bf16[1,368,256]{2,1,0:T(8,128)(2,1)S(1)}, bf16[1,184,256]{2,1,0:T(8,128)(2,1)S(1)}, f32[3,1,3]{2,1,0:T(1,128)S(1)}) custom-call(bf16[1,360,256]{2,1,0:T(8,128)(2,1)} %rays_ref.1, s32[2,1,16]{2,1,0:T(1,128)} %bitcast.12, s32[2,1,16]{2,1,0:T(1,128)} %bitcast.13, f32[3,1,3]{2,1,0:T(1,128)} %bitcast.11), custom_call_target="tpu_custom_call" | custom-call | tf_op jit(solution)/shard_map/prepare/pallas_call | solution.py:357
  1.6 4.1 %collective-permute-start.6 = (bf16[1,184,256]{2,1,0:T(8,128)(2,1)S(1)}, bf16[1,184,256]{2,1,0:T(8,128)(2,1)S(1)}, u32[]{:S(2)}, u32[]{:S(2)}) collective-permute-start(bf16[1,184,256]{2,1,0:T(8,128)(2,1)S(1)} %get-tuple-element.25.refs_1_), channel_id=1, source_target_pairs={{0,16},{1,17},{2,18},{3,19},{4,20},{5,21},{6,22},{7,23},{8,24},{9,... | collective-permute-start | bytes 282632 | tf_op jit(solution)/shard_map/ppermute | solution.py:351
  5.8 1.6 %collective-permute-start.4 = (bf16[1,184,256]{2,1,0:T(8,128)(2,1)S(1)}, bf16[1,184,256]{2,1,0:T(8,128)(2,1)S(1)}, u32[]{:S(2)}, u32[]{:S(2)}) collective-permute-start(bf16[1,184,256]{2,1,0:T(8,128)(2,1)S(1)} %get-tuple-element.25.refs_1_), channel_id=1, source_target_pairs={{0,8},{1,9},{2,10},{3,11},{4,12},{5,13},{6,14},{7,15},{8,0},{9,1},... | collective-permute-start | bytes 282632 | tf_op jit(solution)/shard_map/ppermute | solution.py:351
  7.4 0.0 collective-permute-start.3
  7.4 0.0 collective-permute-start.1
  7.4 2.7 %collective-permute-start.8 = (bf16[1,368,256]{2,1,0:T(8,128)(2,1)S(1)}, bf16[1,368,256]{2,1,0:T(8,128)(2,1)S(1)}, u32[]{:S(2)}, u32[]{:S(2)}) collective-permute-start(bf16[1,368,256]{2,1,0:T(8,128)(2,1)S(1)} %get-tuple-element.24.refs_0_.refs_3_), channel_id=1, source_target_pairs={{0,5},{1,4},{2,7},{3,6},{4,1},{5,0},{6,3},{7,2},{8,13},{9,12},{10,... | collective-permute-start | bytes 565256 | tf_op jit(solution)/shard_map/ppermute | solution.py:351
  10.0 0.3 collective-permute-done.6.refs_5_
  10.3 1.8 %collective-permute-start.9 = (bf16[1,368,256]{2,1,0:T(8,128)(2,1)S(1)}, bf16[1,368,256]{2,1,0:T(8,128)(2,1)S(1)}, u32[]{:S(2)}, u32[]{:S(2)}) collective-permute-start(bf16[1,368,256]{2,1,0:T(8,128)(2,1)S(1)} %get-tuple-element.24.refs_0_.refs_3_), channel_id=1, source_target_pairs={{0,4},{1,5},{2,6},{3,7},{4,0},{5,1},{6,2},{7,3},{8,12},{9,13},{10,... | collective-permute-start | bytes 565256 | tf_op jit(solution)/shard_map/ppermute | solution.py:351
  12.1 0.0 collective-permute-done.4.refs_3_
  12.1 0.0 collective-permute-start.7
  12.1 0.0 collective-permute-done.3.refs_2_
  12.1 1.6 %collective-permute-start = (bf16[1,368,256]{2,1,0:T(8,128)(2,1)S(1)}, bf16[1,368,256]{2,1,0:T(8,128)(2,1)S(1)}, u32[]{:S(2)}, u32[]{:S(2)}) collective-permute-start(bf16[1,368,256]{2,1,0:T(8,128)(2,1)S(1)} %get-tuple-element.24.refs_0_.refs_3_), channel_id=1, source_target_pairs={{0,1},{1,0},{2,3},{3,2},{4,5},{5,4},{6,7},{7,6},{8,9},{9,8},{10,11... | collective-permute-start | bytes 565256 | tf_op jit(solution)/shard_map/ppermute | solution.py:351
  13.7 0.7 %collective-permute-done.1.refs_1_ = bf16[1,184,256]{2,1,0:T(8,128)(2,1)S(1)} collective-permute-done((bf16[1,184,256]{2,1,0:T(8,128)(2,1)S(1)}, bf16[1,184,256]{2,1,0:T(8,128)(2,1)S(1)}, u32[]{:S(2)}, u32[]{:S(2)}) %collective-permute-start.1) | collective-permute-done | bytes 94240 | tf_op jit(solution)/shard_map/ppermute | solution.py:351
  14.4 0.5 %collective-permute-start.2 = (bf16[1,184,256]{2,1,0:T(8,128)(2,1)S(1)}, bf16[1,184,256]{2,1,0:T(8,128)(2,1)S(1)}, u32[]{:S(2)}, u32[]{:S(2)}) collective-permute-start(bf16[1,184,256]{2,1,0:T(8,128)(2,1)S(1)} %collective-permute-done.1.refs_1_), channel_id=1, source_target_pairs={{0,2},{1,3},{2,0},{3,1},{4,6},{5,7},{6,4},{7,5},{8,10},{9,11},{10,... | collective-permute-start | bytes 282632 | tf_op jit(solution)/shard_map/ppermute | solution.py:351
  14.9 0.8 %collective-permute-done.5.refs_4_ = bf16[1,184,256]{2,1,0:T(8,128)(2,1)S(1)} collective-permute-done((bf16[1,184,256]{2,1,0:T(8,128)(2,1)S(1)}, bf16[1,184,256]{2,1,0:T(8,128)(2,1)S(1)}, u32[]{:S(2)}, u32[]{:S(2)}) %collective-permute-start.5) | collective-permute-done | bytes 94240 | tf_op jit(solution)/shard_map/ppermute | solution.py:351
  15.7 0.7 %shard_map.59 = (bf16[1,368,256]{2,1,0:T(8,128)(2,1)S(1)}, f32[1,360,256]{2,1,0:T(8,128)S(1)}, f32[1,256]{1,0:T(1,128)S(1)}, f32[2,1,6,128]{3,2,1,0:T(8,128)S(1)...) custom-call(bf16[1,368,256]{2,1,0:T(8,128)(2,1)S(1)} %get-tuple-element.24.refs_0_.refs_3_, ...), custom_call_target="tpu_custom_call" | custom-call | tf_op jit(solution)/shard_map/pallas_call | solution.py:412
  16.4 0.6 %shard_map.60 = (bf16[1,368,256]{2,1,0:T(8,128)(2,1)S(1)}, f32[1,360,256]{2,1,0:T(8,128)S(1)}, f32[1,256]{1,0:T(1,128)S(1)}, f32[2,1,6,128]{3,2,1,0:T(8,128)S(1)}) custom-call(bf16[1,368,256]{2,1,0:T(8,128)(2,1)S(1)} %collective-permute-done.8.refs_0_, bf16[6,192,256]{2,1,0:T(8,128)(2,1)S(1)} %get-tuple-element.30.refs_1_.refs_15_, ...), custom_call_target="tpu_custom_call" | custom-call | tf_op jit(solution)/shard_map/pallas_call | solution.py:412
  17.0 2.5 %collective-permute-done.9.refs_0_ = bf16[1,368,256]{2,1,0:T(8,128)(2,1)S(1)} collective-permute-done((bf16[1,368,256]{2,1,0:T(8,128)(2,1)S(1)}, bf16[1,368,256]{2,1,0:T(8,128)(2,1)S(1)}, u32[]{:S(2)}, u32[]{:S(2)}) %collective-permute-start.9) | collective-permute-done | bytes 188448 | tf_op jit(solution)/shard_map/ppermute | solution.py:351
  19.5 0.7 %shard_map.61 = (bf16[1,368,256]{2,1,0:T(8,128)(2,1)S(1)}, f32[1,360,256]{2,1,0:T(8,128)S(1)}, f32[1,256]{1,0:T(1,128)S(1)}, f32[2,1,6,128]{3,2,1,0:T(8,128)S(1)...) custom-call(bf16[1,368,256]{2,1,0:T(8,128)(2,1)S(1)} %collective-permute-done.9.refs_0_, ...), custom_call_target="tpu_custom_call" | custom-call | tf_op jit(solution)/shard_map/pallas_call | solution.py:412
  20.1 0.0 collective-permute-done.2.refs_2_
  20.1 0.0 collective-permute-done.refs_0_
  20.2 1.3 %last.1 = f32[32,1,128]{2,1,0:T(1,128)S(1)} custom-call(bf16[1,368,256]{2,1,0:T(8,128)(2,1)S(1)} %collective-permute-done.refs_0_, bf16[1,184,256]{2,1,0:T(8,128)(2,1)S(1)} %collective-permute-done.1.refs_1_, bf16[1,184,256]{2,1,0:T(8,128)(2,1)S(1)} %collective-permute-done.2.refs_2_, bf16[1,368,256]{2,1,0:T(8,128)(2,1)S(1)} %get-tuple-element.26.refs_3_, ...), custom_call_target="tpu_custom_call" | custom-call | tf_op jit(solution)/shard_map/last/pallas_call | solution.py:427
  21.4 12.3 %all_to_all.5.gathered_ref = f32[32,1,128]{2,1,0:T(1,128)S(1)} all-to-all(f32[32,1,128]{2,1,0:T(1,128)S(1)} %last.1), channel_id=1, replica_groups=mesh['row'=16,'col'=2] {'row','col'}, dimensions={0} | all-to-all | bytes 32768 | tf_op jit(solution)/shard_map/all_to_all | solution.py:443
  33.8 1.9 %power.1 = (f32[2,1,16]{2,1,0:T(1,128)}, f32[3,1,3]{2,1,0:T(1,128)}) custom-call(f32[32,1,128]{2,1,0:T(1,128)S(1)} %all_to_all.5.gathered_ref), custom_call_target="tpu_custom_call" | custom-call | tf_op jit(solution)/shard_map/power/pallas_call | solution.py:445
  (3 shorter events, 0.0 us)
Async XLA Ops:
  1.6 8.7 %collective-permute-start.6 = (bf16[1,184,256]{2,1,0:T(8,128)(2,1)S(1)}, bf16[1,184,256]{2,1,0:T(8,128)(2,1)S(1)}, u32[]{:S(2)}, u32[]{:S(2)}) collective-permute-start(bf16[1,184,256]{2,1,0:T(8,128)(2,1)S(1)} %get-tuple-element.25.refs_1_), channel_id=1, source_target_pairs={{0,16},{1,17},{2,18},{3,19},{4,20},{5,21},{6,22},{7,23},{8,24},{9,... | collective-permute-start | bytes 282632 | tf_op jit(solution)/shard_map/ppermute | solution.py:351
  5.8 6.3 %collective-permute-start.4 = (bf16[1,184,256]{2,1,0:T(8,128)(2,1)S(1)}, bf16[1,184,256]{2,1,0:T(8,128)(2,1)S(1)}, u32[]{:S(2)}, u32[]{:S(2)}) collective-permute-start(bf16[1,184,256]{2,1,0:T(8,128)(2,1)S(1)} %get-tuple-element.25.refs_1_), channel_id=1, source_target_pairs={{0,8},{1,9},{2,10},{3,11},{4,12},{5,13},{6,14},{7,15},{8,0},{9,1},... | collective-permute-start | bytes 282632 | tf_op jit(solution)/shard_map/ppermute | solution.py:351
  7.4 4.7 %collective-permute-start.3 = (bf16[1,184,256]{2,1,0:T(8,128)(2,1)S(1)}, bf16[1,184,256]{2,1,0:T(8,128)(2,1)S(1)}, u32[]{:S(2)}, u32[]{:S(2)}) collective-permute-start(bf16[1,184,256]{2,1,0:T(8,128)(2,1)S(1)} %get-tuple-element.25.refs_1_), channel_id=1, source_target_pairs={{0,2},{1,3},{2,0},{3,1},{4,6},{5,7},{6,4},{7,5},{8,10},{9,11},{10,... | collective-permute-start | bytes 282632 | tf_op jit(solution)/shard_map/ppermute | solution.py:351
  7.4 7.0 %collective-permute-start.1 = (bf16[1,184,256]{2,1,0:T(8,128)(2,1)S(1)}, bf16[1,184,256]{2,1,0:T(8,128)(2,1)S(1)}, u32[]{:S(2)}, u32[]{:S(2)}) collective-permute-start(bf16[1,184,256]{2,1,0:T(8,128)(2,1)S(1)} %get-tuple-element.25.refs_1_), channel_id=1, source_target_pairs={{0,24},{1,25},{2,26},{3,27},{4,28},{5,29},{6,30},{7,31},{8,16},{9,... | collective-permute-start | bytes 282632 | tf_op jit(solution)/shard_map/ppermute | solution.py:351
  7.4 9.0 %collective-permute-start.8 = (bf16[1,368,256]{2,1,0:T(8,128)(2,1)S(1)}, bf16[1,368,256]{2,1,0:T(8,128)(2,1)S(1)}, u32[]{:S(2)}, u32[]{:S(2)}) collective-permute-start(bf16[1,368,256]{2,1,0:T(8,128)(2,1)S(1)} %get-tuple-element.24.refs_0_.refs_3_), channel_id=1, source_target_pairs={{0,5},{1,4},{2,7},{3,6},{4,1},{5,0},{6,3},{7,2},{8,13},{9,12},{10,... | collective-permute-start | bytes 565256 | tf_op jit(solution)/shard_map/ppermute | solution.py:351
  10.3 9.2 %collective-permute-start.9 = (bf16[1,368,256]{2,1,0:T(8,128)(2,1)S(1)}, bf16[1,368,256]{2,1,0:T(8,128)(2,1)S(1)}, u32[]{:S(2)}, u32[]{:S(2)}) collective-permute-start(bf16[1,368,256]{2,1,0:T(8,128)(2,1)S(1)} %get-tuple-element.24.refs_0_.refs_3_), channel_id=1, source_target_pairs={{0,4},{1,5},{2,6},{3,7},{4,0},{5,1},{6,2},{7,3},{8,12},{9,13},{10,... | collective-permute-start | bytes 565256 | tf_op jit(solution)/shard_map/ppermute | solution.py:351
  12.1 2.3 %collective-permute-start.7 = (bf16[1,184,256]{2,1,0:T(8,128)(2,1)S(1)}, bf16[1,184,256]{2,1,0:T(8,128)(2,1)S(1)}, u32[]{:S(2)}, u32[]{:S(2)}) collective-permute-start(bf16[1,184,256]{2,1,0:T(8,128)(2,1)S(1)} %collective-permute-done.6.refs_5_), channel_id=1, source_target_pairs={{0,2},{1,3},{2,0},{3,1},{4,6},{5,7},{6,4},{7,5},{8,10},{9,11},{10,... | collective-permute-start | bytes 282632 | tf_op jit(solution)/shard_map/ppermute | solution.py:351
  12.1 8.1 %collective-permute-start = (bf16[1,368,256]{2,1,0:T(8,128)(2,1)S(1)}, bf16[1,368,256]{2,1,0:T(8,128)(2,1)S(1)}, u32[]{:S(2)}, u32[]{:S(2)}) collective-permute-start(bf16[1,368,256]{2,1,0:T(8,128)(2,1)S(1)} %get-tuple-element.24.refs_0_.refs_3_), channel_id=1, source_target_pairs={{0,1},{1,0},{2,3},{3,2},{4,5},{5,4},{6,7},{7,6},{8,9},{9,8},{10,11... | collective-permute-start | bytes 565256 | tf_op jit(solution)/shard_map/ppermute | solution.py:351
  14.4 1.3 %collective-permute-start.5 = (bf16[1,184,256]{2,1,0:T(8,128)(2,1)S(1)}, bf16[1,184,256]{2,1,0:T(8,128)(2,1)S(1)}, u32[]{:S(2)}, u32[]{:S(2)}) collective-permute-start(bf16[1,184,256]{2,1,0:T(8,128)(2,1)S(1)} %collective-permute-done.4.refs_3_), channel_id=1, source_target_pairs={{0,2},{1,3},{2,0},{3,1},{4,6},{5,7},{6,4},{7,5},{8,10},{9,11},{10,... | collective-permute-start | bytes 282632 | tf_op jit(solution)/shard_map/ppermute | solution.py:351
  14.4 5.8 %collective-permute-start.2 = (bf16[1,184,256]{2,1,0:T(8,128)(2,1)S(1)}, bf16[1,184,256]{2,1,0:T(8,128)(2,1)S(1)}, u32[]{:S(2)}, u32[]{:S(2)}) collective-permute-start(bf16[1,184,256]{2,1,0:T(8,128)(2,1)S(1)} %collective-permute-done.1.refs_1_), channel_id=1, source_target_pairs={{0,2},{1,3},{2,0},{3,1},{4,6},{5,7},{6,4},{7,5},{8,10},{9,11},{10,... | collective-permute-start | bytes 282632 | tf_op jit(solution)/shard_map/ppermute | solution.py:351
